TPU v7x, 256 devices: a whole 4x4x8 slice. The times are simulated.
256 devices in a mesh: dom: 8 (over y, core), feat: 32 (over z, x).
Axes of the slice: x: 4, y: 4, z: 8, core: 2. Of those that a mesh axis runs over, the one named last changes fastest.
Arguments:
- node_feats: bfloat16 [1024, 32768], P('feat', 'dom'), may hold values from -6 to 6
- send_rows: int32 [8192], P('dom'), may hold values from 0 to 4095
- hub_rows: int32 [1024], P('dom'), may hold values from 0 to 4095
- tile_dst: int32 [4096], P('dom'), may hold values from 0 to 7
- tile_src: int32 [4096], P('dom'), may hold values from 0 to 47
- tile_count: int32 [8], P('dom'), may hold values from 128 to 512, as said below
- tile_vals: bfloat16 [4096, 128, 128], P('dom'), may hold values from -0.0625 to 0.0625
- w_self: bfloat16 [1024, 1024], P('feat'), may hold values from -0.1875 to 0.1875
- w_neigh: bfloat16 [1024, 1024], P('feat'), may hold values from -0.1875 to 0.1875
- bias_vec: float32 [1024], P('feat'), may hold values from -3 to 3
- cotangent: bfloat16 [1024, 8192], P('feat', 'dom'), may hold values from -6 to 6
Outputs:
- activations: bfloat16 [1024, 8192], P('feat', 'dom')
- grad_feats: float32 [1024, 32768], P('feat', 'dom')
- grad_w_self: float32 [1024, 1024], P('feat')
- grad_w_neigh: float32 [1024, 1024], P('feat')
- grad_bias: float32 [1024], P('feat')
Inputs may be any that keep to these rules, and one draw needn't show every extreme that they name: `tile_count`: every partition has at least 128 live slots, and some partition has all 512 live; slots at or past the count are not edges: their tile_vals may hold any values and must be ignored.
All inputs are finite; a program needn't handle non-finite values.
Results may differ from a plain program's by a relative error of at most 0.0075.
Values may be sent and summed in bfloat16 or wider, within the bound.
A program may use at most 128 MiB of HBM per device.

v0:
```python
import jax
import jax.numpy as jnp
from jax import lax
from jax.sharding import PartitionSpec as P


def contract_first(left, right):
    return lax.dot_general(
        left, right, (((0,), (0,)), ((), ())), preferred_element_type=jnp.float32
    )


def contract_last(left, right):
    return lax.dot_general(
        left, right, (((1,), (1,)), ((), ())), preferred_element_type=jnp.float32
    )


def body(
    node_feats,
    send_rows,
    hub_rows,
    tile_dst,
    tile_src,
    tile_count,
    tile_vals,
    w_self,
    w_neigh,
    bias_vec,
    cotangent,
):
    feat_cols = node_feats.shape[0]
    own_rows = node_feats.shape[1]
    dst_rows = cotangent.shape[1]
    sent_total = send_rows.shape[0]
    outgoing = jnp.take(node_feats, send_rows, axis=1)
    halo_cols = lax.all_to_all(outgoing, "dom", split_axis=1, concat_axis=1, tiled=True)
    hub_cols = lax.all_gather(jnp.take(node_feats, hub_rows, axis=1), "dom", axis=1, tiled=True)
    source_table = jnp.concatenate([node_feats, halo_cols, hub_cols], axis=1)
    tile_total = source_table.shape[1] // 128
    dst_tiles = dst_rows // 128
    live_mask = (jnp.arange(tile_dst.shape[0]) < tile_count[0]).astype(jnp.float32)
    dst_hot = (tile_dst[:, None] == jnp.arange(dst_tiles)[None, :]).astype(jnp.float32) * live_mask[
        :, None
    ]
    src_hot = (tile_src[:, None] == jnp.arange(tile_total)[None, :]).astype(
        jnp.float32
    ) * live_mask[:, None]
    picked = source_table.reshape(feat_cols, tile_total, 128)[:, tile_src, :]
    products = jnp.einsum("fkj,kij->fki", picked, tile_vals, preferred_element_type=jnp.float32)
    summed = jnp.einsum("fki,ku->fui", products, dst_hot, precision=lax.Precision.HIGHEST)
    aggregate = summed.reshape(feat_cols, dst_rows).astype(jnp.bfloat16)
    dst_feats = node_feats[:, :dst_rows]
    whole_self, whole_agg = (
        lax.all_gather(dst_feats, "feat", axis=0, tiled=True),
        lax.all_gather(aggregate, "feat", axis=0, tiled=True),
    )
    pre_act = (
        jnp.dot(w_self, whole_self, preferred_element_type=jnp.float32)
        + jnp.dot(w_neigh, whole_agg, preferred_element_type=jnp.float32)
        + bias_vec[:, None]
    )
    sig_val = jax.nn.sigmoid(pre_act)
    activations = (pre_act * sig_val).astype(jnp.bfloat16)
    grad_pre = (cotangent.astype(jnp.float32) * sig_val * (1.0 + pre_act * (1.0 - sig_val))).astype(
        jnp.bfloat16
    )
    local_self = contract_last(grad_pre, whole_self)
    local_neigh = contract_last(grad_pre, whole_agg)
    local_bias = jnp.sum(grad_pre.astype(jnp.float32), axis=1)
    grad_w_self, grad_w_neigh, grad_bias = lax.psum((local_self, local_neigh, local_bias), "dom")
    both_grads = lax.psum_scatter(
        jnp.concatenate(
            [contract_first(w_self, grad_pre), contract_first(w_neigh, grad_pre)], axis=1
        ),
        "feat",
        scatter_dimension=0,
        tiled=True,
    )
    grad_self_in = both_grads[:, :dst_rows]
    grad_agg = both_grads[:, dst_rows:].astype(jnp.bfloat16)
    upstream = grad_agg.reshape(feat_cols, dst_tiles, 128)[:, tile_dst, :]
    back_terms = jnp.einsum("fki,kij->fkj", upstream, tile_vals, preferred_element_type=jnp.float32)
    placed = jnp.einsum("fkj,kt->ftj", back_terms, src_hot, precision=lax.Precision.HIGHEST)
    grad_table = placed.reshape(feat_cols, tile_total * 128)
    halo_grad = grad_table[:, own_rows : own_rows + sent_total]
    hub_grad = grad_table[:, own_rows + sent_total :]
    returned = lax.all_to_all(
        halo_grad.astype(jnp.bfloat16), "dom", split_axis=1, concat_axis=1, tiled=True
    ).astype(halo_grad.dtype)
    hub_total = lax.psum_scatter(
        hub_grad.astype(jnp.bfloat16), "dom", scatter_dimension=1, tiled=True
    ).astype(jnp.float32)
    grad_feats = grad_table[:, :own_rows]
    grad_feats = grad_feats.at[:, send_rows].add(returned)
    grad_feats = grad_feats.at[:, hub_rows].add(hub_total)
    grad_feats = grad_feats.at[:, :dst_rows].add(grad_self_in)
    return (activations, grad_feats, grad_w_self, grad_w_neigh, grad_bias)


def solution(mesh):
    return jax.shard_map(
        body,
        mesh=mesh,
        in_specs=(
            P("feat", "dom"),
            P("dom"),
            P("dom"),
            P("dom"),
            P("dom"),
            P("dom"),
            P("dom", None, None),
            P("feat", None),
            P("feat", None),
            P("feat"),
            P("feat", "dom"),
        ),
        out_specs=(P("feat", "dom"), P("feat", "dom"), P("feat", None), P("feat", None), P("feat")),
        check_vma=False,
    )
```

profile of v0, /device:TPU:1, one launch (start us, length us, event | category | flops | bytes accessed | tf_op | source)
XLA Modules:
  0.0 554.2 jit_solution(6041104265866286545)
XLA Ops:
  10.9 3.2 gather_fusion
  15.5 6.5 %all-to-all-start = ((bf16[32,8,128]{2,0,1:T(8,128)(2,1)}), bf16[32,8,128]{2,0,1:T(8,128)(2,1)S(1)}, u32[]{:S(2)}, u32[]{:S(2)}) async-start(bf16[32,8,128]{2,0,1:T(8,128)(2,1)} %broadcast_select_fusion), calls=%async_computation | async-start | bytes 131072 | tf_op jit(solution)/shard_map/all_to_all | solution.py:37
  24.8 13.5 %all_gather.10 = bf16[32,1024]{0,1:T(8,128)(2,1)S(1)} all-gather(bf16[32,128]{0,1:T(8,128)(2,1)S(1)} %select_bitcast_fusion), channel_id=1, replica_groups=mesh['dom'=8,'feat'=32] {'dom'}, dimensions={1}, use_global_device_ids=true | all-gather | bytes 73728 | tf_op jit(solution)/shard_map/all_gather | solution.py:38
  40.2 3.5 gather_fusion.2
  43.7 13.0 %fusion.8 = f32[32,512,128]{2,0,1:T(8,128)S(1)} fusion(bf16[512,128,128]{2,1,0:T(8,128)(2,1)} %param.19, bf16[512,32,128]{2,1,0:T(8,128)(2,1)} %gather_fusion.2), kind=kOutput, calls=%fused_computation.15 | convolution fusion | flops 536870912 | bytes 29360128 | tf_op jit(solution)/shard_map/fkj,kij->fki/dot_general | solution.py:50
  56.7 8.6 %fusion.16 = bf16[8,32,128]{2,0,1:T(8,128)(2,1)S(1)} fusion(f32[32,512,128]{2,0,1:T(8,128)S(1)} %fusion.8, f32[512]{0:T(512)S(1)} %fusion.30, s32[512]{0:T(512)S(1)} %copy-done.6), kind=kOutput, calls=%fused_computation.22 | convolution fusion | flops 201367552 | bytes 8458240 | tf_op jit(solution)/shard_map/fki,ku->fui/dot_general | solution.py:51
  66.2 22.8 %all-gather.3.cloned.1.call-done = bf16[1024,1024]{1,0:T(8,128)(2,1)} async-done(((bf16[32,1024]{1,0:T(8,128)(2,1)}), bf16[1024,1024]{1,0:T(8,128)(2,1)}) %all-gather.3.cloned.1.call-update) | async-done | bytes 2097168 | tf_op jit(solution)/shard_map/all_gather | solution.py:55
  89.0 2.1 fusion.35
  91.0 76.2 %all-gather.5.cloned.1.call-done = bf16[1024,1024]{1,0:T(8,128)(2,1)} async-done(((bf16[32,1024]{1,0:T(8,128)(2,1)}), bf16[1024,1024]{1,0:T(8,128)(2,1)}) %all-gather.5.cloned.1.call-update) | async-done | bytes 2097168 | tf_op jit(solution)/shard_map/all_gather | solution.py:56
  167.3 2.8 convert_reduce_fusion
  171.6 4.1 pad_maximum_fusion
  175.7 9.2 %copy.95 = f32[1024,2048]{1,0:T(8,128)} copy(f32[1024,2048]{0,1:T(8,128)} %pad_maximum_fusion) | data formatting | bytes 16777216
  187.8 223.5 %reduce-scatter.7.cloned.1.call-done = f32[32,2048]{1,0:T(8,128)} async-done(((f32[1024,2048]{1,0:T(8,128)}), f32[32,2048]{1,0:T(8,128)}) %reduce-scatter.7.cloned.1.call-update) | async-done | bytes 262160
  412.5 3.5 gather_fusion.3
  416.0 9.3 %fusion.11 = f32[32,512,128]{2,0,1:T(8,128)S(1)} fusion(bf16[512,128,128]{2,1,0:T(8,128)(2,1)} %param.19, bf16[512,32,128]{2,1,0:T(8,128)(2,1)} %gather_fusion.3), kind=kOutput, calls=%fused_computation.16 | convolution fusion | flops 536870912 | bytes 29360128 | tf_op jit(solution)/shard_map/fki,kij->fkj/dot_general | solution.py:83
  425.3 9.6 %fusion = f32[48,32,128]{2,0,1:T(8,128)S(1)} fusion(f32[32,512,128]{2,0,1:T(8,128)S(1)} %fusion.11, f32[512]{0:T(512)S(1)} %fusion.30, s32[512]{0:T(512)S(1)} %copy-done.7), kind=kOutput, calls=%fused_computation.7 | convolution fusion | flops 1208008704 | bytes 9179136 | tf_op jit(solution)/shard_map/fkj,kt->ftj/dot_general | solution.py:84
  435.9 8.8 %all-to-all-start.1 = ((bf16[32,8,128]{2,0,1:T(8,128)(2,1)}), bf16[32,8,128]{2,0,1:T(8,128)(2,1)S(1)}, u32[]{:S(2)}, u32[]{:S(2)}) async-start(bf16[32,8,128]{2,0,1:T(8,128)(2,1)} %bitcast.91), calls=%async_computation.1 | async-start | bytes 131072 | tf_op jit(solution)/shard_map/all_to_all | solution.py:88
  447.1 12.7 %psum.23 = f32[32]{0:T(128)} all-reduce(f32[32]{0:T(128)S(1)} %get-tuple-element.54), channel_id=1, replica_groups=mesh['dom'=8,'feat'=32] {'dom'}, use_global_device_ids=true, to_apply=%region_8.9 | all-reduce | flops 32 | bytes 256 | tf_op jit(solution)/shard_map/psum | solution.py:71
  461.1 7.0 %scatter_fusion = f32[32,4096]{0,1:T(8,128)S(1)} fusion(f32[32,4096]{0,1:T(8,128)S(1)} %copy.99, s32[1024]{0:T(1024)S(1)} %get-tuple-element.59, f32[1024,32]{1,0:T(8,128)S(1)} %copy.90), kind=kCustom, calls=%fused_computation.4 | custom fusion | flops 32768 | bytes 397312 | tf_op jit(solution)/shard_map/scatter-add | solution.py:95
  468.1 9.4 %reduce-scatter.9.cloned.1.call-done = bf16[128,32]{1,0:T(8,128)(2,1)} async-done(((bf16[1024,32]{1,0:T(8,128)(2,1)}), bf16[128,32]{1,0:T(8,128)(2,1)}) %reduce-scatter.9.cloned.1.call-update) | async-done | bytes 8208
  478.4 2.0 scatter_fusion.1
  482.6 61.9 %all-reduce.3.cloned.1.call-done = (f32[32,1024]{1,0:T(8,128)}, f32[32,1024]{1,0:T(8,128)}) async-done(((f32[32,1024]{1,0:T(8,128)}, f32[32,1024]{1,0:T(8,128)}), (f32[32,1024]{1,0:T(8,128)}, f32[32,1024]{1,0:T(8,128)})) %all-reduce.3.cloned.1.call-update) | async-done | bytes 262160 | tf_op jit(solution)/shard_map/psum | solution.py:71
  544.6 1.6 copy.132
  546.1 1.6 copy.133
  (75 shorter events, 23.3 us)
Async XLA Ops:
  7.2 160.1 %copy-start = (bf16[32,1024]{1,0:T(8,128)(2,1)S(1)}, bf16[32,1024]{1,0:T(8,128)(2,1)}, u32[]{:S(2)}) copy-start(bf16[32,1024]{1,0:T(8,128)(2,1)} %param.21) | copy-start | bytes 196612
  7.2 81.8 %all-gather.3.cloned.1.call-start = ((), (), s32[]{:S(2)}) async-start(), calls=%async_computation.4 | async-start | bytes 2162688 | tf_op jit(solution)/shard_map/all_gather | solution.py:55
  15.5 23.7 %all-to-all-start = ((bf16[32,8,128]{2,0,1:T(8,128)(2,1)}), bf16[32,8,128]{2,0,1:T(8,128)(2,1)S(1)}, u32[]{:S(2)}, u32[]{:S(2)}) async-start(bf16[32,8,128]{2,0,1:T(8,128)(2,1)} %broadcast_select_fusion), calls=%async_computation | async-start | bytes 131072 | tf_op jit(solution)/shard_map/all_to_all | solution.py:37
  22.0 145.3 %all-gather.5.cloned.1.call-start = ((), (), s32[]{:S(2)}) async-start(), calls=%async_computation.5 | async-start | bytes 2162688 | tf_op jit(solution)/shard_map/all_gather | solution.py:56
  43.7 13.0 %copy-start.6 = (s32[512]{0:T(512)S(1)}, s32[512]{0:T(512)}, u32[]{:S(2)}) copy-start(s32[512]{0:T(512)} %param.16) | copy-start | bytes 6148
  56.7 32.3 %copy-start.4 = (bf16[32,1024]{1,0:T(8,128)(2,1)S(1)}, bf16[32,1024]{1,0:T(8,128)(2,1)}, u32[]{:S(2)}) copy-start(bf16[32,1024]{1,0:T(8,128)(2,1)} %param.20) | copy-start | bytes 196612
  56.7 110.6 %copy-start.5 = (bf16[32,1024]{1,0:T(8,128)(2,1)S(1)}, bf16[32,1024]{1,0:T(8,128)(2,1)}, u32[]{:S(2)}) copy-start(bf16[32,1024]{1,0:T(8,128)(2,1)} %param.23) | copy-start | bytes 196612
  56.7 110.6 %copy-start.8 = (f32[32]{0:T(128)S(1)}, f32[32]{0:T(128)}, u32[]{:S(2)}) copy-start(f32[32]{0:T(128)} %param.22) | copy-start | bytes 388
  66.0 345.3 %reduce-scatter.7.cloned.1.call-start = ((), (), s32[]{:S(2)}) async-start(), calls=%async_computation.6 | async-start | bytes 8650752
  184.9 1.6 copy-start.3
  416.0 9.3 %copy-start.7 = (s32[512]{0:T(512)S(1)}, s32[512]{0:T(512)}, u32[]{:S(2)}) copy-start(s32[512]{0:T(512)} %param.17) | copy-start | bytes 6148
  425.3 20.3 %copy-start.2 = (bf16[1024,1024]{1,0:T(8,128)(2,1)S(1)}, bf16[1024,1024]{1,0:T(8,128)(2,1)}, u32[]{:S(2)}) copy-start(bf16[1024,1024]{1,0:T(8,128)(2,1)} %all-gather.3.cloned.1.call-done) | copy-start | bytes 6291460
  435.0 25.0 %slice-start = ((f32[32,2048]{1,0:T(8,128)}), f32[32,1024]{1,0:T(8,128)S(1)}, s32[]{:S(2)}) async-start(f32[32,2048]{1,0:T(8,128)} %reduce-scatter.7.cloned.1.call-done), calls=%async_computation.9 | async-start | bytes 262144 | tf_op jit(solution)/shard_map/slice | solution.py:80
  435.9 25.0 %all-to-all-start.1 = ((bf16[32,8,128]{2,0,1:T(8,128)(2,1)}), bf16[32,8,128]{2,0,1:T(8,128)(2,1)S(1)}, u32[]{:S(2)}, u32[]{:S(2)}) async-start(bf16[32,8,128]{2,0,1:T(8,128)(2,1)} %bitcast.91), calls=%async_computation.1 | async-start | bytes 131072 | tf_op jit(solution)/shard_map/all_to_all | solution.py:88
  444.7 32.8 %reduce-scatter.9.cloned.1.call-start = ((), (), s32[]{:S(2)}) async-start(), calls=%async_computation.7 | async-start | bytes 294912
  445.6 99.0 %all-reduce.3.cloned.1.call-start = ((), (), s32[]{:S(2)}) async-start(), calls=%async_computation.8 | async-start | bytes 524288 | tf_op jit(solution)/shard_map/psum | solution.py:71
  460.2 87.5 %copy-start.1 = (bf16[32,1024]{1,0:T(8,128)(2,1)S(1)}, bf16[32,1024]{1,0:T(8,128)(2,1)}, u32[]{:S(2)}) copy-start(bf16[32,1024]{1,0:T(8,128)(2,1)} %param.21) | copy-start | bytes 196612
Sparse Core Ops, SparseCore 0:
  11.2 77.7 all-gather.2
  92.1 75.1 all-gather.4
  185.0 226.2 reduce-scatter.6
  448.5 28.9 reduce-scatter.8
  480.3 64.2 all-reduce.2
where the time goes:
time: 556 us; the launch traced here: 554 us
  waiting for transfers between devices  394 us (71%)
  matrix products  49.7 us (9%)
  local copies, waits for them, and re-layouts  34.4 us (6%)
  blocking collectives  26.2 us (5%)
  other arithmetic  19.8 us (4%)
  starting transfers between devices  15.6 us (3%)
  between operations  14.7 us (3%)
    unnamed x7, waiting for transfers between devices  233 us
    all_gather x1, waiting for transfers between devices, body(): lax.all_gather(aggregate, 'feat', axis=0, tiled=True)  76.2 us
    psum x1, waiting for transfers between devices, body(): lax.psum((local_self, local_neigh, local_bias), 'dom')  61.9 us
    all_gather x1, waiting for transfers between devices, body(): lax.all_gather(dst_feats, 'feat', axis=0, tiled=True)  22.8 us
    unnamed x31, local copies, waits for them, and re-layouts  19.8 us
    all_gather x1, blocking collectives, body(): lax.all_gather(jnp.take(node_feats, hub_rows, axis=1), 'dom', axis=1, til...  13.5 us
    dot_general x1, matrix products, body(): jnp.einsum('fkj,kij->fki', picked, tile_vals, preferred_element_type=jnp....  13 us
    psum x1, blocking collectives, body(): lax.psum((local_self, local_neigh, local_bias), 'dom')  12.7 us
  transfers between devices with their start and end apart: 7, of which 5 were waited for; matrix products, arithmetic and copies ran while one was open for 10% of the time, Pallas kernels for 0%

commit v1 on v0

v1 whole, which is shorter than its diff:
```python
import functools

import jax
import jax.numpy as jnp
from jax import lax
from jax.experimental import pallas as pl
from jax.experimental.pallas import tpu as pltpu
from jax.sharding import PartitionSpec as P

MESH = pl.DeviceIdType.MESH
F32 = jnp.float32
BF16 = jnp.bfloat16
ZH = 4
LANES = 128
VMEM_LIMIT = 48 * 1024 * 1024


def remote(src, dst, send_sem, recv_sem, where):
    return pltpu.make_async_remote_copy(
        src_ref=src,
        dst_ref=dst,
        send_sem=send_sem,
        recv_sem=recv_sem,
        device_id=where,
        device_id_type=MESH,
    )


def place(near):
    dom = lax.axis_index("dom")
    feat = lax.axis_index("feat")
    return dom, feat, lax.div(feat, near), lax.rem(feat, near)


def aligned(index, size):
    return pl.ds(pl.multiple_of(index * size, size), size)


def column_hot(index_row):
    low = jnp.bitwise_and(index_row, LANES - 1)
    rows = lax.broadcasted_iota(jnp.int32, (LANES, LANES), 0)
    return jnp.where(rows == low, 1.0, 0.0).astype(BF16)


def distribute_kernel(
    doms,
    near,
    feats_ref,
    send_ref,
    hub_ref,
    w_self_ref,
    w_neigh_ref,
    bias_ref,
    cot_ref,
    table,
    wrow,
    wcol,
    x_self,
    cot_part,
    bias_part,
    picked,
    w_both,
    w_regrouped,
    bias_wide,
    halo_s,
    halo_r,
    hub_s,
    hub_r,
    far_s,
    far_r,
    near_s,
    near_r,
    col_s,
    col_r,
    share_s,
    share_r,
):
    rows = feats_ref.shape[0]
    own_tiles = feats_ref.shape[1] // LANES
    width = w_self_ref.shape[1]
    chunk = width // doms
    quarter = cot_ref.shape[1] // ZH
    feat_total = ZH * near
    dom, feat, zh, nr = place(near)

    barrier = pltpu.get_barrier_semaphore()
    for i in range(1, doms):
        pl.semaphore_signal(
            barrier, inc=1, device_id={"dom": lax.rem(dom + i, doms)}, device_id_type=MESH
        )
    for i in range(1, ZH):
        pl.semaphore_signal(
            barrier,
            inc=1,
            device_id={"feat": lax.rem(zh + i, ZH) * near + nr},
            device_id_type=MESH,
        )
    for i in range(1, near):
        pl.semaphore_signal(
            barrier,
            inc=1,
            device_id={"feat": zh * near + lax.rem(nr + i, near)},
            device_id_type=MESH,
        )

    @pl.when(nr != dom)
    def _():
        for i in range(1, ZH):
            pl.semaphore_signal(
                barrier,
                inc=1,
                device_id={"feat": lax.rem(zh + i, ZH) * near + dom},
                device_id_type=MESH,
            )

    for t in range(own_tiles):
        table[t] = feats_ref[:, t * LANES : (t + 1) * LANES]
    stacked = table[0:own_tiles].reshape(own_tiles * rows, LANES)
    for block in range(doms + 1):
        index_row = hub_ref[...] if block == doms else send_ref[block : block + 1, :]
        high = jnp.right_shift(index_row, 7)
        found = jnp.dot(stacked, column_hot(index_row), preferred_element_type=F32)
        found = found.reshape(own_tiles, rows, LANES)
        total = jnp.zeros((rows, LANES), F32)
        for t in range(own_tiles):
            total = total + jnp.where(high == t, found[t], 0.0)
        picked[block] = total.astype(BF16)

    common = (doms - 1) + (ZH - 1) + (near - 1)

    @pl.when(nr == dom)
    def _():
        pl.semaphore_wait(barrier, common + (ZH - 1) * (near - 1))

    @pl.when(nr != dom)
    def _():
        pl.semaphore_wait(barrier, common)

    def halo_copy(i, source, target):
        return remote(
            picked.at[target],
            table.at[own_tiles + source],
            halo_s.at[i],
            halo_r.at[i],
            {"dom": target},
        )

    def hub_copy(i, source, target):
        return remote(
            picked.at[doms],
            table.at[own_tiles + doms + source],
            hub_s.at[i],
            hub_r.at[i],
            {"dom": target},
        )

    for i in range(1, doms):
        target = lax.rem(dom + i, doms)
        halo_copy(i, dom, target).start()
        hub_copy(i, dom, target).start()

    def far_copies(i, source, target):
        where = {"feat": target * near + nr}
        return (
            remote(
                feats_ref.at[:, aligned(target, quarter)],
                x_self.at[source, nr],
                far_s.at[0, i],
                far_r.at[0, i],
                where,
            ),
            remote(
                w_both.at[:, :, aligned(dom, chunk)],
                wrow.at[:, source, :, aligned(dom, chunk)],
                far_s.at[1, i],
                far_r.at[1, i],
                where,
            ),
            remote(
                cot_ref.at[:, aligned(target, quarter)],
                cot_part.at[source],
                far_s.at[2, i],
                far_r.at[2, i],
                where,
            ),
            remote(
                bias_wide,
                bias_part.at[source],
                far_s.at[3, i],
                far_r.at[3, i],
                where,
            ),
        )

    w_both[0] = w_self_ref[...]
    w_both[1] = w_neigh_ref[...]
    spot = lax.broadcasted_iota(jnp.int32, (rows, rows), 0)
    lane = lax.broadcasted_iota(jnp.int32, (rows, rows), 1)
    bias_column = jnp.sum(jnp.where(spot == lane, bias_ref[...], 0.0), axis=1, keepdims=True)
    bias_wide[...] = jnp.broadcast_to(bias_column, (rows, LANES))
    for i in range(1, ZH):
        for copy in far_copies(i, zh, lax.rem(zh + i, ZH)):
            copy.start()

    lanes_at = lax.broadcasted_iota(jnp.int32, (rows, LANES), 1)
    for m, w_ref in enumerate((w_self_ref, w_neigh_ref)):
        for n in range(near):
            joined = jnp.zeros((rows, LANES), F32)
            for h in range(ZH):
                first = (h * near + n) * rows
                base, offset = first // LANES * LANES, first % LANES
                piece = w_ref[:, base : base + LANES].astype(F32)
                shift = (h * rows - offset) % LANES
                if shift:
                    piece = pltpu.roll(piece, shift, 1)
                inside = (lanes_at >= h * rows) & (lanes_at < (h + 1) * rows)
                joined = jnp.where(inside, piece, joined)
            w_regrouped[n, m] = joined.astype(BF16)

    def col_copy(i, target):
        return remote(
            w_regrouped.at[lax.rem(target, near)],
            wcol.at[:, zh, nr],
            col_s.at[i],
            col_r.at[zh],
            {"feat": target},
        )

    @pl.when(nr == dom)
    def _():
        for i in range(1, feat_total):
            col_copy(i, lax.rem(feat + i, feat_total)).start()
        wcol[:, zh, nr] = w_regrouped[nr]

    x_self[zh, nr] = feats_ref[:, aligned(zh, quarter)]
    wrow[:, zh, :, aligned(dom, chunk)] = w_both[:, :, aligned(dom, chunk)]
    cot_part[zh] = cot_ref[:, aligned(zh, quarter)]
    bias_part[zh] = bias_wide[...]
    table[own_tiles + dom] = picked[dom]
    table[own_tiles + doms + dom] = picked[doms]

    for i in range(1, ZH):
        for copy in far_copies(i, lax.rem(zh + ZH - i, ZH), zh):
            copy.wait_recv()

    def near_copy(i, source, target):
        return remote(
            x_self.at[:, source],
            x_self.at[:, source],
            near_s.at[i],
            near_r.at[i],
            {"feat": zh * near + target},
        )

    for i in range(1, near):
        near_copy(i, nr, lax.rem(nr + i, near)).start()

    for h in range(ZH):

        @pl.when((nr != dom) | (zh != h))
        def _():
            remote(
                w_regrouped.at[0],
                wcol.at[:, h, dom],
                col_s.at[0],
                col_r.at[h],
                {"feat": feat},
            ).wait_recv()

    def share_copies(i, source, target):
        where = {"dom": target}
        return (
            remote(
                wrow.at[:, :, :, aligned(source, chunk)],
                wrow.at[:, :, :, aligned(source, chunk)],
                share_s.at[0, i],
                share_r.at[0, i],
                where,
            ),
            remote(
                wcol.at[:, :, source],
                wcol.at[:, :, source],
                share_s.at[1, i],
                share_r.at[1, i],
                where,
            ),
        )

    for i in range(1, doms):
        for copy in share_copies(i, dom, lax.rem(dom + i, doms)):
            copy.start()

    for i in range(1, doms):
        source = lax.rem(dom + doms - i, doms)
        halo_copy(i, source, dom).wait_recv()
        hub_copy(i, source, dom).wait_recv()
    for i in range(1, near):
        near_copy(i, lax.rem(nr + near - i, near), nr).wait_recv()
    for i in range(1, doms):
        for copy in share_copies(i, lax.rem(dom + doms - i, doms), dom):
            copy.wait_recv()

    for i in range(1, doms):
        target = lax.rem(dom + i, doms)
        halo_copy(i, dom, target).wait_send()
        hub_copy(i, dom, target).wait_send()
        for copy in share_copies(i, dom, target):
            copy.wait_send()
    for i in range(1, ZH):
        for copy in far_copies(i, zh, lax.rem(zh + i, ZH)):
            copy.wait_send()
    for i in range(1, near):
        near_copy(i, nr, lax.rem(nr + i, near)).wait_send()

    @pl.when(nr == dom)
    def _():
        for i in range(1, feat_total):
            col_copy(i, lax.rem(feat + i, feat_total)).wait_send()


def aggregate_kernel(group, src_ref, dst_ref, count_ref, vals_ref, table_ref, out_ref, acc):
    step = pl.program_id(0)
    tiles = acc.shape[0]

    @pl.when(step == 0)
    def _():
        acc[...] = jnp.zeros_like(acc)

    count = count_ref[0]

    @pl.when(step * group < count)
    def _():
        parts = []
        for t in range(group):
            parts.append(
                lax.dot_general(
                    table_ref[src_ref[step * group + t]],
                    vals_ref[t],
                    (((1,), (1,)), ((), ())),
                    preferred_element_type=F32,
                )
            )
        for t in range(group):
            at = dst_ref[step * group + t]
            acc[at] += jnp.where(step * group + t < count, parts[t], 0.0)

    @pl.when(step == pl.num_programs(0) - 1)
    def _():
        for u in range(tiles):
            out_ref[:, u * LANES : (u + 1) * LANES] = acc[u].astype(BF16)


def spread_kernel(
    group, own_tiles, src_ref, dst_ref, count_ref, vals_ref, grad_ref, own_ref, away_ref, acc
):
    step = pl.program_id(0)

    @pl.when(step == 0)
    def _():
        acc[...] = jnp.zeros_like(acc)

    count = count_ref[0]

    @pl.when(step * group < count)
    def _():
        parts = []
        for t in range(group):
            parts.append(
                jnp.dot(
                    grad_ref[dst_ref[step * group + t]],
                    vals_ref[t],
                    preferred_element_type=F32,
                )
            )
        for t in range(group):
            at = src_ref[step * group + t]
            acc[at] += jnp.where(step * group + t < count, parts[t], 0.0)

    @pl.when(step == pl.num_programs(0) - 1)
    def _():
        own_ref[...] = acc[0:own_tiles]
        away_ref[...] = acc[own_tiles:].astype(BF16)


def dense_kernel(
    doms,
    near,
    agg_ref,
    x_self,
    wrow,
    wcol,
    cot_ref,
    bias_ref,
    act_out,
    grad_agg,
    grad_self,
    w_final,
    x_agg,
    g_part,
    g_all,
    act_part,
    in_parts,
    w_parts,
    w_got,
    w_sums,
    w_zh,
    far_s,
    far_r,
    near_s,
    near_r,
    back_s,
    back_r,
    sum_s,
    sum_r,
):
    rows, columns = agg_ref.shape
    quarter = columns // ZH
    halves = quarter // LANES
    width = rows * ZH * near
    mine = ZH * rows
    wide = 2 * width // doms
    dom, feat, zh, nr = place(near)

    barrier = pltpu.get_barrier_semaphore()
    for i in range(1, doms):
        pl.semaphore_signal(
            barrier, inc=1, device_id={"dom": lax.rem(dom + i, doms)}, device_id_type=MESH
        )
    for i in range(1, ZH):
        pl.semaphore_signal(
            barrier,
            inc=1,
            device_id={"feat": lax.rem(zh + i, ZH) * near + nr},
            device_id_type=MESH,
        )
    for i in range(1, near):
        pl.semaphore_signal(
            barrier,
            inc=1,
            device_id={"feat": zh * near + lax.rem(nr + i, near)},
            device_id_type=MESH,
        )
    pl.semaphore_wait(barrier, (doms - 1) + (ZH - 1) + (near - 1))

    def far_copy(i, source, target):
        return remote(
            agg_ref.at[:, aligned(target, quarter)],
            x_agg.at[source, nr],
            far_s.at[i],
            far_r.at[i],
            {"feat": target * near + nr},
        )

    for i in range(1, ZH):
        far_copy(i, zh, lax.rem(zh + i, ZH)).start()
    x_agg[zh, nr] = agg_ref[:, aligned(zh, quarter)]
    pre = jnp.dot(
        wrow[0].reshape(mine, width),
        x_self[...].reshape(width, quarter),
        preferred_element_type=F32,
    )
    for i in range(1, ZH):
        far_copy(i, lax.rem(zh + ZH - i, ZH), zh).wait_recv()

    def near_copy(which, buffer, i, source, target):
        return remote(
            buffer.at[:, source],
            buffer.at[:, source],
            near_s.at[which, i],
            near_r.at[which, i],
            {"feat": zh * near + target},
        )

    for i in range(1, near):
        near_copy(0, x_agg, i, nr, lax.rem(nr + i, near)).start()
    for i in range(1, near):
        near_copy(0, x_agg, i, lax.rem(nr + near - i, near), nr).wait_recv()

    pre = pre + jnp.dot(
        wrow[1].reshape(mine, width),
        x_agg[...].reshape(width, quarter),
        preferred_element_type=F32,
    )
    bias = jnp.concatenate([bias_ref[...].reshape(mine, LANES)] * halves, axis=1)
    pre = pre + bias
    sig = jax.nn.sigmoid(pre)
    grad = cot_ref[...].reshape(mine, quarter).astype(F32) * sig * (1.0 + pre * (1.0 - sig))
    grad = grad.astype(BF16)
    g_part[...] = grad
    g_all[:, nr] = grad.reshape(ZH, rows, quarter)
    for i in range(1, near):
        near_copy(1, g_all, i, nr, lax.rem(nr + i, near)).start()

    act = (pre * sig).astype(BF16).reshape(ZH, rows, quarter)
    for h in range(halves):
        act_part[:, h] = act[:, :, h * LANES : (h + 1) * LANES]

    def back_copy(which, source_buffer, target_buffer, i, source, target):
        return remote(
            source_buffer.at[target],
            target_buffer.at[aligned(source, halves)],
            back_s.at[which, i],
            back_r.at[which, i],
            {"feat": target * near + nr},
        )

    for i in range(1, ZH):
        back_copy(0, act_part, act_out, i, zh, lax.rem(zh + i, ZH)).start()
    act_out[aligned(zh, halves)] = act_part[zh]

    over_x = (((1,), (1,)), ((), ()))
    half_doms = doms // 2
    bias_sum = jnp.sum(grad.astype(F32), axis=1, keepdims=True)
    bias_sum = jnp.broadcast_to(bias_sum, (mine, LANES)).astype(BF16)
    for m, x_ref in enumerate((x_self, x_agg)):
        product = lax.dot_general(
            g_part[...],
            x_ref[...].reshape(width, quarter),
            over_x,
            preferred_element_type=F32,
        ).astype(BF16)
        for d in range(half_doms):
            w_parts[m * half_doms + d, :, 0:wide] = product[:, d * wide : (d + 1) * wide]
    for d in range(doms):
        w_parts[d, :, wide:] = bias_sum

    def sum_copy(i, source, target):
        return remote(
            w_parts.at[target],
            w_got.at[source],
            sum_s.at[0, i],
            sum_r.at[0, i],
            {"dom": target},
        )

    for i in range(1, doms):
        sum_copy(i, dom, lax.rem(dom + i, doms)).start()

    for i in range(1, near):
        near_copy(1, g_all, i, lax.rem(nr + near - i, near), nr).wait_recv()
    over_out = (((0,), (0,)), ((), ()))
    for m, (target_buffer) in ((1, grad_agg), (0, grad_self)):
        back = lax.dot_general(
            wcol[m].reshape(width, mine),
            g_all[...].reshape(width, quarter),
            over_out,
            preferred_element_type=F32,
        )
        back = back.astype(BF16).reshape(ZH, rows, quarter)
        for h in range(halves):
            in_parts[m, :, h] = back[:, :, h * LANES : (h + 1) * LANES]
        for i in range(1, ZH):
            back_copy(
                1 + m, in_parts.at[m], target_buffer, i, zh, lax.rem(zh + i, ZH)
            ).start()
        target_buffer[aligned(zh, halves)] = in_parts[m, zh]

    for i in range(1, doms):
        sum_copy(i, lax.rem(dom + doms - i, doms), dom).wait_recv()
    w_got[dom] = w_parts[dom]
    total = w_got[0].astype(F32)
    for d in range(1, doms):
        total = total + w_got[d].astype(F32)
    w_sums[...] = total.reshape(ZH, rows, wide + LANES)

    def zh_copy(i, source, target):
        return remote(
            w_sums.at[target],
            w_zh.at[source],
            sum_s.at[1, i],
            sum_r.at[1, i],
            {"feat": target * near + nr},
        )

    for i in range(1, ZH):
        zh_copy(i, zh, lax.rem(zh + i, ZH)).start()
    w_zh[zh] = w_sums[zh]
    for i in range(1, ZH):
        zh_copy(i, lax.rem(zh + ZH - i, ZH), zh).wait_recv()
    total = w_zh[0]
    for h in range(1, ZH):
        total = total + w_zh[h]
    w_final[...] = total

    for i in range(1, ZH):
        source = lax.rem(zh + ZH - i, ZH)
        back_copy(0, act_part, act_out, i, source, zh).wait_recv()
        back_copy(1, in_parts.at[0], grad_self, i, source, zh).wait_recv()
        back_copy(2, in_parts.at[1], grad_agg, i, source, zh).wait_recv()
    for i in range(1, ZH):
        target = lax.rem(zh + i, ZH)
        far_copy(i, zh, target).wait_send()
        back_copy(0, act_part, act_out, i, zh, target).wait_send()
        back_copy(1, in_parts.at[0], grad_self, i, zh, target).wait_send()
        back_copy(2, in_parts.at[1], grad_agg, i, zh, target).wait_send()
        zh_copy(i, zh, target).wait_send()
    for i in range(1, near):
        target = lax.rem(nr + i, near)
        near_copy(0, x_agg, i, nr, target).wait_send()
        near_copy(1, g_all, i, nr, target).wait_send()
    for i in range(1, doms):
        sum_copy(i, dom, lax.rem(dom + i, doms)).wait_send()


def return_kernel(
    doms, near, away_ref, w_final, returned, hub_parts, w_all, ret_s, ret_r, hub_s, hub_r, w_s, w_r
):
    dom, feat, zh, nr = place(near)
    wide = w_all.shape[2]
    barrier = pltpu.get_barrier_semaphore()
    for i in range(1, doms):
        pl.semaphore_signal(
            barrier, inc=1, device_id={"dom": lax.rem(dom + i, doms)}, device_id_type=MESH
        )
    pl.semaphore_wait(barrier, doms - 1)

    def copies(i, source, target):
        where = {"dom": target}
        return (
            remote(away_ref.at[target], returned.at[source], ret_s.at[i], ret_r.at[i], where),
            remote(
                away_ref.at[doms + target], hub_parts.at[source], hub_s.at[i], hub_r.at[i], where
            ),
            remote(w_final.at[:, 0:wide], w_all.at[source], w_s.at[i], w_r.at[i], where),
        )

    for i in range(1, doms):
        for copy in copies(i, dom, lax.rem(dom + i, doms)):
            copy.start()
    returned[dom] = away_ref[dom]
    hub_parts[dom] = away_ref[doms + dom]
    w_all[dom] = w_final[:, 0:wide]
    for i in range(1, doms):
        for copy in copies(i, lax.rem(dom + doms - i, doms), dom):
            copy.wait_recv()
    for i in range(1, doms):
        for copy in copies(i, dom, lax.rem(dom + i, doms)):
            copy.wait_send()


def finish_kernel(
    doms,
    own_ref,
    returned_ref,
    hub_ref,
    self_ref,
    send_rows,
    hub_rows,
    w_all,
    w_final,
    act_ref,
    act_out,
    feats_out,
    w_self_out,
    w_neigh_out,
    bias_out,
    masked,
):
    own_tiles, rows, _ = own_ref.shape
    dst_tiles = self_ref.shape[0]
    wide = w_all.shape[2]
    hots = []
    for block in range(doms + 1):
        if block == doms:
            index_row = hub_rows[...]
            total = hub_ref[0].astype(F32)
            for d in range(1, doms):
                total = total + hub_ref[d].astype(F32)
            values = total.astype(BF16)
        else:
            index_row = send_rows[block : block + 1, :]
            values = returned_ref[block]
        high = jnp.right_shift(index_row, 7)
        values = values.astype(F32)
        for t in range(own_tiles):
            masked[t, :, block * LANES : (block + 1) * LANES] = jnp.where(
                high == t, values, 0.0
            ).astype(BF16)
        hots.append(column_hot(index_row))
    hot = jnp.concatenate(hots, axis=1)
    added = lax.dot_general(
        masked[...].reshape(own_tiles * rows, (doms + 1) * LANES),
        hot,
        (((1,), (1,)), ((), ())),
        preferred_element_type=F32,
    ).reshape(own_tiles, rows, LANES)
    for t in range(own_tiles):
        total = own_ref[t] + added[t]
        if t < dst_tiles:
            total = total + self_ref[t].astype(F32)
        feats_out[:, t * LANES : (t + 1) * LANES] = total
    for t in range(dst_tiles):
        act_out[:, t * LANES : (t + 1) * LANES] = act_ref[t]
    half = doms // 2
    for d in range(half):
        w_self_out[:, d * wide : (d + 1) * wide] = w_all[d]
        w_neigh_out[:, d * wide : (d + 1) * wide] = w_all[half + d]
    spot = lax.broadcasted_iota(jnp.int32, (rows, LANES), 0)
    lane = lax.broadcasted_iota(jnp.int32, (rows, LANES), 1)
    picked = jnp.where(spot == lane, w_final[:, wide:], 0.0)
    bias_out[...] = jnp.sum(picked, axis=0, keepdims=True)[:, 0:rows]


def vmem(count):
    return [pl.BlockSpec(memory_space=pltpu.VMEM)] * count


def shape(dims, dtype):
    return jax.ShapeDtypeStruct(dims, dtype)


def body(
    doms,
    feat_total,
    node_feats,
    send_rows,
    hub_rows,
    tile_dst,
    tile_src,
    tile_count,
    tile_vals,
    w_self,
    w_neigh,
    bias_vec,
    cotangent,
):
    near = feat_total // ZH
    rows, own = node_feats.shape
    own_tiles = own // LANES
    columns = cotangent.shape[1]
    dst_tiles = columns // LANES
    quarter = columns // ZH
    width = w_self.shape[1]
    mine = ZH * rows
    wide = 2 * width // doms
    all_tiles = own_tiles + 2 * doms
    tile_total = tile_src.shape[0]
    dma = pltpu.SemaphoreType.DMA

    send_grid = send_rows.reshape(doms, LANES)
    hub_grid = hub_rows.reshape(1, LANES)

    def params(identity):
        return pltpu.CompilerParams(
            collective_id=identity, has_side_effects=True, vmem_limit_bytes=VMEM_LIMIT
        )

    table, wrow, wcol, x_self, cot_part, bias_part = pl.pallas_call(
        functools.partial(distribute_kernel, doms, near),
        name="distribute",
        out_shape=(
            shape((all_tiles, rows, LANES), BF16),
            shape((2, ZH, rows, width), BF16),
            shape((2, ZH, near, rows, mine), BF16),
            shape((ZH, near, rows, quarter), BF16),
            shape((ZH, rows, quarter), BF16),
            shape((ZH, rows, LANES), F32),
        ),
        in_specs=vmem(7),
        out_specs=tuple(vmem(6)),
        scratch_shapes=[
            pltpu.VMEM((doms + 1, rows, LANES), BF16),
            pltpu.VMEM((2, rows, width), BF16),
            pltpu.VMEM((near, 2, rows, mine), BF16),
            pltpu.VMEM((rows, LANES), F32),
            dma((doms,)),
            dma((doms,)),
            dma((doms,)),
            dma((doms,)),
            dma((4, ZH)),
            dma((4, ZH)),
            dma((near,)),
            dma((near,)),
            dma((feat_total,)),
            dma((ZH,)),
            dma((2, doms)),
            dma((2, doms)),
        ],
        compiler_params=params(0),
    )(node_feats, send_grid, hub_grid, w_self, w_neigh, bias_vec.reshape(1, rows), cotangent)

    group = min(32, tile_total)

    def live_block(step, src, dst, count):
        last = lax.div(count[0] + group - 1, group) - 1
        return (jnp.minimum(step, last), 0, 0)

    def whole(rank):
        return lambda step, src, dst, count: (0,) * rank

    vals_spec = pl.BlockSpec((group, LANES, LANES), live_block)
    local = pltpu.CompilerParams(vmem_limit_bytes=VMEM_LIMIT)

    aggregate = pl.pallas_call(
        functools.partial(aggregate_kernel, group),
        name="aggregate",
        out_shape=shape((rows, columns), BF16),
        grid_spec=pltpu.PrefetchScalarGridSpec(
            num_scalar_prefetch=3,
            grid=(tile_total // group,),
            in_specs=[vals_spec, pl.BlockSpec((all_tiles, rows, LANES), whole(3))],
            out_specs=pl.BlockSpec((rows, columns), whole(2)),
            scratch_shapes=[pltpu.VMEM((dst_tiles, rows, LANES), F32)],
        ),
        compiler_params=local,
    )(tile_src, tile_dst, tile_count, tile_vals, table)

    act_tiles, grad_agg, grad_self, w_final = pl.pallas_call(
        functools.partial(dense_kernel, doms, near),
        name="dense",
        out_shape=(
            shape((dst_tiles, rows, LANES), BF16),
            shape((dst_tiles, rows, LANES), BF16),
            shape((dst_tiles, rows, LANES), BF16),
            shape((rows, wide + LANES), F32),
        ),
        in_specs=vmem(6),
        out_specs=tuple(vmem(4)),
        scratch_shapes=[
            pltpu.VMEM((ZH, near, rows, quarter), BF16),
            pltpu.VMEM((mine, quarter), BF16),
            pltpu.VMEM((ZH, near, rows, quarter), BF16),
            pltpu.VMEM((ZH, quarter // LANES, rows, LANES), BF16),
            pltpu.VMEM((2, ZH, quarter // LANES, rows, LANES), BF16),
            pltpu.VMEM((doms, mine, wide + LANES), BF16),
            pltpu.VMEM((doms, mine, wide + LANES), BF16),
            pltpu.VMEM((ZH, rows, wide + LANES), F32),
            pltpu.VMEM((ZH, rows, wide + LANES), F32),
            dma((ZH,)),
            dma((ZH,)),
            dma((2, near)),
            dma((2, near)),
            dma((3, ZH)),
            dma((3, ZH)),
            dma((2, max(doms, ZH))),
            dma((2, max(doms, ZH))),
        ],
        compiler_params=params(1),
    )(aggregate, x_self, wrow, wcol, cot_part, bias_part)

    grad_own, away = pl.pallas_call(
        functools.partial(spread_kernel, group, own_tiles),
        name="spread",
        out_shape=(
            shape((own_tiles, rows, LANES), F32),
            shape((2 * doms, rows, LANES), BF16),
        ),
        grid_spec=pltpu.PrefetchScalarGridSpec(
            num_scalar_prefetch=3,
            grid=(tile_total // group,),
            in_specs=[vals_spec, pl.BlockSpec((dst_tiles, rows, LANES), whole(3))],
            out_specs=(
                pl.BlockSpec((own_tiles, rows, LANES), whole(3)),
                pl.BlockSpec((2 * doms, rows, LANES), whole(3)),
            ),
            scratch_shapes=[pltpu.VMEM((all_tiles, rows, LANES), F32)],
        ),
        compiler_params=local,
    )(tile_src, tile_dst, tile_count, tile_vals, grad_agg)

    returned, hub_parts, w_all = pl.pallas_call(
        functools.partial(return_kernel, doms, near),
        name="give_back",
        out_shape=(
            shape((doms, rows, LANES), BF16),
            shape((doms, rows, LANES), BF16),
            shape((doms, rows, wide), F32),
        ),
        in_specs=vmem(2),
        out_specs=tuple(vmem(3)),
        scratch_shapes=[dma((doms,)) for _ in range(6)],
        compiler_params=params(2),
    )(away, w_final)

    activations, grad_feats, grad_w_self, grad_w_neigh, grad_bias = pl.pallas_call(
        functools.partial(finish_kernel, doms),
        name="finish",
        out_shape=(
            shape((rows, columns), BF16),
            shape((rows, own), F32),
            shape((rows, width), F32),
            shape((rows, width), F32),
            shape((1, rows), F32),
        ),
        in_specs=vmem(9),
        out_specs=tuple(vmem(5)),
        scratch_shapes=[pltpu.VMEM((own_tiles, rows, (doms + 1) * LANES), BF16)],
        compiler_params=local,
    )(
        grad_own,
        returned,
        hub_parts,
        grad_self,
        send_grid,
        hub_grid,
        w_all,
        w_final,
        act_tiles,
    )
    return (activations, grad_feats, grad_w_self, grad_w_neigh, grad_bias.reshape(rows))


def solution(mesh):
    return jax.shard_map(
        functools.partial(body, mesh.shape["dom"], mesh.shape["feat"]),
        mesh=mesh,
        in_specs=(
            P("feat", "dom"),
            P("dom"),
            P("dom"),
            P("dom"),
            P("dom"),
            P("dom"),
            P("dom", None, None),
            P("feat", None),
            P("feat", None),
            P("feat"),
            P("feat", "dom"),
        ),
        out_specs=(P("feat", "dom"), P("feat", "dom"), P("feat", None), P("feat", None), P("feat")),
        check_vma=False,
    )
```

time: 556 us -> 122 us (0.22)
  waiting for transfers between devices: 394 us -> 0 us
  Pallas kernels: 0 us -> 113 us
  matrix products: 49.7 us -> 0 us
  local copies, waits for them, and re-layouts: 34.4 us -> 6.83 us
  blocking collectives: 26.2 us -> 0 us
  other arithmetic: 19.8 us -> 0 us
  starting transfers between devices: 15.6 us -> 0 us
  between operations: 14.7 us -> 1.39 us
    unnamed x7 -> x0, waiting for transfers between devices: 233 us -> none
    pallas_call x0 -> x6, Pallas kernels: none -> 113 us  [the longest x1 38.5 us: body(): pl.pallas_call(functools.partial(distribute_kernel, doms, near), name='di...]
    all_gather x2 -> x0, waiting for transfers between devices: 99 us -> none  [the longest x1 76.2 us: body(): lax.all_gather(aggregate, 'feat', axis=0, tiled=True)]
    psum x1 -> x0, waiting for transfers between devices: 61.9 us -> none  [body(): lax.psum((local_self, local_neigh, local_bias), 'dom')]
    dot_general x10 -> x0, matrix products: 49.7 us -> none  [the longest x1 13 us: body(): jnp.einsum('fkj,kij->fki', picked, tile_vals, preferred_element_type=jnp....]
    all_to_all x2 -> x0, starting transfers between devices: 15.3 us -> none  [the longest x1 8.82 us: body(): lax.all_to_all(halo_grad.astype(jnp.bfloat16), 'dom', split_axis=1, conca...]
    all_gather x1 -> x0, blocking collectives: 13.5 us -> none  [body(): lax.all_gather(jnp.take(node_feats, hub_rows, axis=1), 'dom', axis=1, til...]
    unnamed x31 -> x22, local copies, waits for them, and re-layouts: 19.8 us -> 6.83 us
  transfers between devices with their start and end apart: 7 -> 0, of which waited for: 5 -> 0; matrix products, arithmetic and copies ran while one was open for 10% -> 0% of each run, Pallas kernels for 0% -> 0%
where the time goes in v1:
time: 122 us; the launch traced here: 121 us
  Pallas kernels  113 us (93%)
  local copies, waits for them, and re-layouts  6.83 us (6%)
  between operations  1.39 us (1%)
    pallas_call x1, Pallas kernels, body(): pl.pallas_call(functools.partial(distribute_kernel, doms, near), name='di...  38.5 us
    pallas_call x1, Pallas kernels, body(): pl.pallas_call(functools.partial(dense_kernel, doms, near), name='dense',...  36.7 us
    pallas_call x1, Pallas kernels, body(): pl.pallas_call(functools.partial(return_kernel, doms, near), name='give_b...  15.1 us
    pallas_call x1, Pallas kernels, body(): pl.pallas_call(functools.partial(aggregate_kernel, group), name='aggregat...  11.3 us
    pallas_call x1, Pallas kernels, body(): pl.pallas_call(functools.partial(spread_kernel, group, own_tiles), name='...  9.89 us
    unnamed x22, local copies, waits for them, and re-layouts  6.83 us

profile of v1, /device:TPU:1, one launch (start us, length us, event | category | flops | bytes accessed | tf_op | source)
XLA Modules:
  0.0 121.3 jit_solution(16571689948506916770)
XLA Ops:
  0.6 0.0 copy-start.6
  0.6 0.0 copy-start.8
  1.3 0.0 copy-start
  1.3 0.9 copy-done
  2.3 0.0 copy-start.1
  2.3 0.8 copy-done.1
  3.1 0.0 copy-start.2
  3.1 0.8 copy-done.2
  4.0 0.0 copy-start.3
  4.0 0.8 copy-done.3
  4.8 0.7 copy-done.4
  5.5 0.7 copy-done.9
  6.1 0.7 copy-done.10
  6.8 38.5 %distribute.1 = (bf16[48,32,128]{2,1,0:T(8,128)(2,1)S(1)}, bf16[2,4,32,1024]{3,2,1,0:T(8,128)(2,1)S(1)}, bf16[2,4,8,32,128]{4,3,2,1,0:T(8,128)(2,1)S(1)}, bf16[4...) custom-call(bf16[32,4096]{1,0:T(8,128)(2,1)S(1)} %copy-done, ...), custom_call_target="tpu_custom_call" | custom-call | tf_op jit(solution)/shard_map/distribute/pallas_call | solution.py:748
  45.3 0.0 copy-start.5
  45.3 0.7 copy-done.5
  46.0 0.7 copy-done.7
  46.6 11.3 %aggregate.1.agg_ref = bf16[32,1024]{1,0:T(8,128)(2,1)S(1)} custom-call(s32[512]{0:T(512)S(1)} %copy-done.5, s32[512]{0:T(512)S(1)} %copy-done.7, s32[1]{0:T(128)S(6)} %copy.16.count_ref, bf16[512,128,128]{2,1,0:T(8,128)(2,1)} %vals_ref.3, bf16[48,32,128]{2,1,0:T(8,128)(2,1)S(1)} %get-tuple-element.25.table_ref), custom_call_target="tpu_custom_call" | custom-call | tf_op jit(solution)/shard_map/aggregate/pallas_call | solution.py:794
  57.9 36.7 %dense.1 = (bf16[8,32,128]{2,1,0:T(8,128)(2,1)S(1)}, bf16[8,32,128]{2,1,0:T(8,128)(2,1)S(1)}, bf16[8,32,128]{2,1,0:T(8,128)(2,1)S(1)}, f32[32,384]{1,0:T(8,128)S(1)}) custom-call(bf16[32,1024]{1,0:T(8,128)(2,1)S(1)} %aggregate.1.agg_ref, bf16[4,8,32,256]{3,2,1,0:T(8,128)(2,1)S(1)} %get-tuple-element.26.x_self, ...), custom_call_target="tpu_custom_call" | custom-call | tf_op jit(solution)/shard_map/dense/pallas_call | solution.py:808
  94.7 0.0 copy-done.6
  94.7 0.0 copy-done.8
  94.7 9.9 %spread.1 = (f32[32,32,128]{2,1,0:T(8,128)S(1)}, bf16[16,32,128]{2,1,0:T(8,128)(2,1)S(1)}) custom-call(s32[512]{0:T(512)S(1)} %copy-done.6, s32[512]{0:T(512)S(1)} %copy-done.8, s32[1]{0:T(128)S(6)} %copy.16.count_ref, bf16[512,128,128]{2,1,0:T(8,128)(2,1)} %vals_ref.3, bf16[8,32,128]{2,1,0:T(8,128)(2,1)S(1)} %get-tuple-element.31.grad_ref), custom_call_target="tpu_custom_call" | custom-call | tf_op jit(solution)/shard_map/spread/pallas_call | solution.py:841
  104.6 15.1 %give_back.1 = (bf16[8,32,128]{2,1,0:T(8,128)(2,1)S(1)}, bf16[8,32,128]{2,1,0:T(8,128)(2,1)S(1)}, f32[8,32,256]{2,1,0:T(8,128)S(1)}) custom-call(bf16[16,32,128]{2,1,0:T(8,128)(2,1)S(1)} %get-tuple-element.33.away_ref, f32[32,384]{1,0:T(8,128)S(1)} %get-tuple-element.34.w_final), custom_call_target="tpu_custom_call" | custom-call | tf_op jit(solution)/shard_map/give_back/pallas_call | solution.py:861
  119.6 1.7 %finish.1 = (bf16[32,1024]{1,0:T(8,128)(2,1)}, f32[32,4096]{1,0:T(8,128)}, f32[32,1024]{1,0:T(8,128)}, f32[32,1024]{1,0:T(8,128)}, f32[1,32]{1,0:T(1,128)}) custom-call(f32[32,32,128]{2,1,0:T(8,128)S(1)} %get-tuple-element.32.own_ref, bf16[8,32,128]{2,1,0:T(8,128)(2,1)S(1)} %get-tuple-element.35.returned_ref, ...), custom_call_target="tpu_custom_call" | custom-call | tf_op jit(solution)/shard_map/finish/pallas_call | solution.py:875
  (4 shorter events, 0.0 us)
Async XLA Ops:
  0.6 94.0 %copy-start.6 = (s32[512]{0:T(512)S(1)}, s32[512]{0:T(512)}, u32[]{:S(2)}) copy-start(s32[512]{0:T(512)} %src_ref.3) | copy-start | bytes 6148
  0.6 94.0 %copy-start.8 = (s32[512]{0:T(512)S(1)}, s32[512]{0:T(512)}, u32[]{:S(2)}) copy-start(s32[512]{0:T(512)} %dst_ref.3) | copy-start | bytes 6148
  1.3 1.0 copy-start
  2.3 0.8 copy-start.1
  3.1 0.8 copy-start.2
  4.0 0.8 copy-start.3
  4.8 0.7 copy-start.4
  5.5 0.7 copy-start.9
  6.1 0.7 copy-start.10
  45.3 0.7 copy-start.5
  46.0 0.7 copy-start.7

commit v2 on v0

v2 whole, which is shorter than its diff:
```python
import functools

import jax
import jax.numpy as jnp
from jax import lax
from jax.experimental import pallas as pl
from jax.experimental.pallas import tpu as pltpu
from jax.sharding import PartitionSpec as P

MESH = pl.DeviceIdType.MESH
F32 = jnp.float32
BF16 = jnp.bfloat16
ZH = 4
LANES = 128
VMEM_LIMIT = 60 * 1024 * 1024
SUB = 64


def remote(src, dst, send_sem, recv_sem, where):
    return pltpu.make_async_remote_copy(
        src_ref=src,
        dst_ref=dst,
        send_sem=send_sem,
        recv_sem=recv_sem,
        device_id=where,
        device_id_type=MESH,
    )


def place(near):
    dom = lax.axis_index("dom")
    feat = lax.axis_index("feat")
    return dom, feat, lax.div(feat, near), lax.rem(feat, near)


def aligned(index, size):
    return pl.ds(pl.multiple_of(index * size, size), size)


def column_hot(index_row):
    low = jnp.bitwise_and(index_row, LANES - 1)
    rows = lax.broadcasted_iota(jnp.int32, (LANES, LANES), 0)
    return jnp.where(rows == low, 1.0, 0.0).astype(BF16)


def link_tiles(keys, count, links, first_row, last_row):
    blocks = keys.shape[0]
    none = blocks * LANES
    above = lax.broadcasted_iota(jnp.int32, (LANES, LANES), 0)
    lane = lax.broadcasted_iota(jnp.int32, (LANES, LANES), 1)
    spread = [
        jnp.transpose(jnp.broadcast_to(keys[b : b + 1, :], (LANES, LANES))) for b in range(blocks)
    ]
    for c in range(blocks):
        best = jnp.full((1, LANES), -1, jnp.int32)
        for b in range(c + 1):
            same = spread[b] == keys[c : c + 1, :]
            if b == c:
                same = same & (above < lane)
            found = jnp.where(same, above + b * LANES, -1)
            best = jnp.maximum(best, jnp.max(found, axis=0, keepdims=True))
        links[first_row + c : first_row + c + 1, :] = jnp.where(best < 0, none, best)
    best = jnp.full((1, LANES), -1, jnp.int32)
    for b in range(blocks):
        same = (spread[b] == lane) & (above + b * LANES < count)
        found = jnp.where(same, above + b * LANES, -1)
        best = jnp.maximum(best, jnp.max(found, axis=0, keepdims=True))
    links[last_row : last_row + 1, :] = jnp.where(best < 0, none, best)


def layer_kernel(
    doms,
    near,
    count_ref,
    feats_hbm,
    send_hbm,
    hub_hbm,
    dst_hbm,
    src_hbm,
    vals_hbm,
    w_self_hbm,
    w_neigh_hbm,
    bias_hbm,
    cot_hbm,
    act_out,
    grad_own,
    returned,
    w_all,
    w_final,
    feats,
    send,
    hub,
    dst,
    src,
    vals,
    flipped,
    runs,
    links,
    links_s,
    table,
    picked,
    w_both,
    w_regrouped,
    bias,
    bias_wide,
    bias_part,
    cot,
    cot_part,
    wrow,
    wcol,
    x_self,
    x_agg,
    agg,
    g_part,
    g_all,
    act_part,
    in_parts,
    grad_agg,
    grad_self,
    away,
    w_parts,
    w_got,
    w_sums,
    w_zh,
    load_sem,
    vals_sem,
    link_sem,
    halo_s,
    halo_r,
    far_s,
    far_r,
    near_s,
    near_r,
    col_s,
    col_r,
    share_s,
    share_r,
    agg_s,
    agg_r,
    back_s,
    back_r,
    sum_s,
    sum_r,
    ret_s,
    ret_r,
):
    rows = feats.shape[0]
    own_tiles = feats.shape[1] // LANES
    columns = cot.shape[1]
    dst_tiles = columns // LANES
    quarter = columns // ZH
    halves = quarter // LANES
    width = w_both.shape[2]
    chunk = width // doms
    mine = ZH * rows
    wide = 2 * width // doms
    tile_total = vals.shape[0]
    key_rows = tile_total // LANES
    feat_total = ZH * near
    dom, feat, zh, nr = place(near)

    barrier = pltpu.get_barrier_semaphore()
    for i in range(1, doms):
        pl.semaphore_signal(
            barrier, inc=1, device_id={"dom": lax.rem(dom + i, doms)}, device_id_type=MESH
        )
    for i in range(1, ZH):
        pl.semaphore_signal(
            barrier,
            inc=1,
            device_id={"feat": lax.rem(zh + i, ZH) * near + nr},
            device_id_type=MESH,
        )
    for i in range(1, near):
        pl.semaphore_signal(
            barrier,
            inc=1,
            device_id={"feat": zh * near + lax.rem(nr + i, near)},
            device_id_type=MESH,
        )

    @pl.when(nr != dom)
    def _():
        for i in range(1, ZH):
            pl.semaphore_signal(
                barrier,
                inc=1,
                device_id={"feat": lax.rem(zh + i, ZH) * near + dom},
                device_id_type=MESH,
            )

    loads = [
        pltpu.make_async_copy(source, target, load_sem.at[i])
        for i, (source, target) in enumerate(
            (
                (feats_hbm, feats),
                (send_hbm, send),
                (hub_hbm, hub),
                (dst_hbm, dst),
                (src_hbm, src),
                (w_self_hbm, w_both.at[0]),
                (w_neigh_hbm, w_both.at[1]),
                (bias_hbm, bias),
                (cot_hbm, cot),
            )
        )
    ]
    for load in loads:
        load.start()
    blocks = vals_sem.shape[0]
    block = tile_total // blocks
    vals_loads = [
        pltpu.make_async_copy(
            vals_hbm.at[b * block : (b + 1) * block],
            vals.at[b * block : (b + 1) * block],
            vals_sem.at[b],
        )
        for b in range(blocks)
    ]
    for load in vals_loads:
        load.start()
    for load in loads:
        load.wait()

    for t in range(own_tiles):
        table[t] = feats[:, t * LANES : (t + 1) * LANES]
    stacked = table[0:own_tiles].reshape(own_tiles * rows, LANES)
    for reader in range(doms + 1):
        index_row = hub[...] if reader == doms else send[reader : reader + 1, :]
        high = jnp.right_shift(index_row, 7)
        found = jnp.dot(stacked, column_hot(index_row), preferred_element_type=F32)
        found = found.reshape(own_tiles, rows, LANES)
        total = jnp.zeros((rows, LANES), F32)
        for t in range(own_tiles):
            total = total + jnp.where(high == t, found[t], 0.0)
        total = total.astype(BF16)
        if reader < doms:
            picked[reader, 0] = total
        else:
            for d in range(doms):
                picked[d, 1] = total

    common = (doms - 1) + (ZH - 1) + (near - 1)

    @pl.when(nr == dom)
    def _():
        pl.semaphore_wait(barrier, common + (ZH - 1) * (near - 1))

    @pl.when(nr != dom)
    def _():
        pl.semaphore_wait(barrier, common)

    def halo_copy(i, source, target):
        return remote(
            picked.at[target],
            table.at[pl.ds(own_tiles + 2 * source, 2)],
            halo_s.at[i],
            halo_r.at[i],
            {"dom": target},
        )

    for i in range(1, doms):
        halo_copy(i, dom, lax.rem(dom + i, doms)).start()

    def far_copy(which, i, source, target):
        sources = (
            feats.at[:, aligned(target, quarter)],
            w_both.at[:, :, aligned(dom, chunk)],
            cot.at[:, aligned(target, quarter)],
            bias_wide,
        )
        targets = (
            x_self.at[source, nr],
            wrow.at[:, source, :, aligned(dom, chunk)],
            cot_part.at[source],
            bias_part.at[source],
        )
        return remote(
            sources[which],
            targets[which],
            far_s.at[which, i],
            far_r.at[which, i],
            {"feat": target * near + nr},
        )

    for i in range(1, ZH):
        far_copy(0, i, zh, lax.rem(zh + i, ZH)).start()
    for i in range(1, ZH):
        far_copy(1, i, zh, lax.rem(zh + i, ZH)).start()

    lanes_at = lax.broadcasted_iota(jnp.int32, (rows, LANES), 1)
    for m in range(2):
        for n in range(near):
            joined = jnp.zeros((rows, LANES), F32)
            for h in range(ZH):
                first = (h * near + n) * rows
                base, offset = first // LANES * LANES, first % LANES
                piece = w_both[m, :, base : base + LANES].astype(F32)
                shift = (h * rows - offset) % LANES
                if shift:
                    piece = pltpu.roll(piece, shift, 1)
                inside = (lanes_at >= h * rows) & (lanes_at < (h + 1) * rows)
                joined = jnp.where(inside, piece, joined)
            w_regrouped[n, m] = joined.astype(BF16)

    def col_copy(i, target):
        return remote(
            w_regrouped.at[lax.rem(target, near)],
            wcol.at[:, zh, nr],
            col_s.at[i],
            col_r.at[zh],
            {"feat": target},
        )

    @pl.when(nr == dom)
    def _():
        for i in range(1, feat_total):
            col_copy(i, lax.rem(feat + i, feat_total)).start()
        wcol[:, zh, nr] = w_regrouped[nr]

    spot = lax.broadcasted_iota(jnp.int32, (rows, rows), 0)
    lane = lax.broadcasted_iota(jnp.int32, (rows, rows), 1)
    bias_column = jnp.sum(jnp.where(spot == lane, bias[...], 0.0), axis=1, keepdims=True)
    bias_wide[...] = jnp.broadcast_to(bias_column, (rows, LANES))
    for which in (2, 3):
        for i in range(1, ZH):
            far_copy(which, i, zh, lax.rem(zh + i, ZH)).start()

    x_self[zh, nr] = feats[:, aligned(zh, quarter)]
    wrow[:, zh, :, aligned(dom, chunk)] = w_both[:, :, aligned(dom, chunk)]
    cot_part[zh] = cot[:, aligned(zh, quarter)]
    bias_part[zh] = bias_wide[...]
    table[pl.ds(own_tiles + 2 * dom, 2)] = picked[dom]

    given = src[...]
    outside = given - own_tiles
    placed = own_tiles + 2 * lax.rem(outside, doms) + lax.div(outside, doms)
    placed = jnp.where(outside < 0, given, placed)
    key_dst = dst[...]
    links[0:key_rows, :] = key_dst
    links[key_rows : 2 * key_rows, :] = placed
    prev_dst, prev_src, last_dst = 2 * key_rows, 3 * key_rows, 4 * key_rows
    last_src = last_dst + 1
    link_tiles(key_dst, count_ref[0], links, prev_dst, last_dst)
    link_tiles(placed, count_ref[0], links, prev_src, last_src)
    link_copy = pltpu.make_async_copy(links, links_s, link_sem)
    link_copy.start()

    def flip(b):
        vals_loads[b].wait()

        def some(j, carry):
            for t in range(8):
                k = b * block + j * 8 + t
                flipped[k] = jnp.transpose(vals[k])
            return carry

        lax.fori_loop(0, block // 8, some, 0)

    early = blocks // 4
    for b in range(early):
        flip(b)

    for which in (0, 1):
        for i in range(1, ZH):
            far_copy(which, i, lax.rem(zh + ZH - i, ZH), zh).wait_recv()

    def near_copy(which, i, source, target):
        buffer = (x_self, x_agg, g_all)[which]
        return remote(
            buffer.at[:, source],
            buffer.at[:, source],
            near_s.at[which, i],
            near_r.at[which, i],
            {"feat": zh * near + target},
        )

    for i in range(1, near):
        near_copy(0, i, nr, lax.rem(nr + i, near)).start()

    for h in range(ZH):

        @pl.when((nr != dom) | (zh != h))
        def _():
            remote(
                w_regrouped.at[0],
                wcol.at[:, h, dom],
                col_s.at[0],
                col_r.at[h],
                {"feat": feat},
            ).wait_recv()

    def share_copy(which, i, source, target):
        part = wcol.at[:, :, source] if which else wrow.at[:, :, :, aligned(source, chunk)]
        return remote(part, part, share_s.at[which, i], share_r.at[which, i], {"dom": target})

    for which in (0, 1):
        for i in range(1, doms):
            share_copy(which, i, dom, lax.rem(dom + i, doms)).start()

    for b in range(early, blocks):
        flip(b)
    link_copy.wait()
    for i in range(1, doms):
        halo_copy(i, lax.rem(dom + doms - i, doms), dom).wait_recv()

    runs[tile_total] = jnp.zeros((rows, LANES), F32)

    def chain(left, left_row, tiles, prev_row):
        def some(j, carry):
            row = lax.div(j * SUB, LANES)
            start = lax.rem(j * SUB, LANES)
            for t in range(SUB):
                product = jnp.dot(
                    left[links_s[left_row + row, start + t]],
                    tiles[j * SUB + t],
                    preferred_element_type=F32,
                )
                runs[j * SUB + t] = runs[links_s[prev_row + row, start + t]] + product
            return carry

        lax.fori_loop(0, tile_total // SUB, some, 0)

    chain(table, key_rows, flipped, prev_dst)
    for u in range(dst_tiles):
        agg[:, u * LANES : (u + 1) * LANES] = runs[links_s[last_dst, u]].astype(BF16)

    def agg_copy(i, source, target):
        return remote(
            agg.at[:, aligned(target, quarter)],
            x_agg.at[source, nr],
            agg_s.at[i],
            agg_r.at[i],
            {"feat": target * near + nr},
        )

    for i in range(1, ZH):
        agg_copy(i, zh, lax.rem(zh + i, ZH)).start()
    x_agg[zh, nr] = agg[:, aligned(zh, quarter)]
    for i in range(1, near):
        near_copy(0, i, lax.rem(nr + near - i, near), nr).wait_recv()
    for i in range(1, doms):
        share_copy(0, i, lax.rem(dom + doms - i, doms), dom).wait_recv()
    pre = jnp.dot(
        wrow[0].reshape(mine, width),
        x_self[...].reshape(width, quarter),
        preferred_element_type=F32,
    )
    for i in range(1, ZH):
        agg_copy(i, lax.rem(zh + ZH - i, ZH), zh).wait_recv()
    for i in range(1, near):
        near_copy(1, i, nr, lax.rem(nr + i, near)).start()
    for which in (2, 3):
        for i in range(1, ZH):
            far_copy(which, i, lax.rem(zh + ZH - i, ZH), zh).wait_recv()
    bias_all = jnp.concatenate([bias_part[...].reshape(mine, LANES)] * halves, axis=1)
    pre = pre + bias_all
    for i in range(1, near):
        near_copy(1, i, lax.rem(nr + near - i, near), nr).wait_recv()
    pre = pre + jnp.dot(
        wrow[1].reshape(mine, width),
        x_agg[...].reshape(width, quarter),
        preferred_element_type=F32,
    )
    sig = jax.nn.sigmoid(pre)
    grad = cot_part[...].reshape(mine, quarter).astype(F32) * sig * (1.0 + pre * (1.0 - sig))
    grad = grad.astype(BF16)
    g_part[...] = grad
    g_all[:, nr] = grad.reshape(ZH, rows, quarter)
    for i in range(1, near):
        near_copy(2, i, nr, lax.rem(nr + i, near)).start()

    act = (pre * sig).astype(BF16).reshape(ZH, rows, quarter)
    for h in range(halves):
        act_part[:, h] = act[:, :, h * LANES : (h + 1) * LANES]

    def back_copy(which, i, source, target):
        source_buffer = (act_part, in_parts.at[0], in_parts.at[1])[which]
        target_buffer = (act_out, grad_self, grad_agg)[which]
        return remote(
            source_buffer.at[target],
            target_buffer.at[aligned(source, halves)],
            back_s.at[which, i],
            back_r.at[which, i],
            {"feat": target * near + nr},
        )

    over_x = (((1,), (1,)), ((), ()))
    half_doms = doms // 2
    bias_sum = jnp.sum(grad.astype(F32), axis=1, keepdims=True)
    bias_sum = jnp.broadcast_to(bias_sum, (mine, LANES)).astype(BF16)
    for m, x_ref in enumerate((x_self, x_agg)):
        product = lax.dot_general(
            g_part[...],
            x_ref[...].reshape(width, quarter),
            over_x,
            preferred_element_type=F32,
        ).astype(BF16)
        for d in range(half_doms):
            w_parts[m * half_doms + d, :, 0:wide] = product[:, d * wide : (d + 1) * wide]
    for d in range(doms):
        w_parts[d, :, wide:] = bias_sum

    def sum_copy(i, source, target):
        return remote(
            w_parts.at[target],
            w_got.at[source],
            sum_s.at[0, i],
            sum_r.at[0, i],
            {"dom": target},
        )

    for i in range(1, doms):
        sum_copy(i, dom, lax.rem(dom + i, doms)).start()
    for i in range(1, doms):
        share_copy(1, i, lax.rem(dom + doms - i, doms), dom).wait_recv()

    for i in range(1, near):
        near_copy(2, i, lax.rem(nr + near - i, near), nr).wait_recv()
    over_out = (((0,), (0,)), ((), ()))
    for m, target_buffer in ((1, grad_agg), (0, grad_self)):
        back = lax.dot_general(
            wcol[m].reshape(width, mine),
            g_all[...].reshape(width, quarter),
            over_out,
            preferred_element_type=F32,
        )
        back = back.astype(BF16).reshape(ZH, rows, quarter)
        for h in range(halves):
            in_parts[m, :, h] = back[:, :, h * LANES : (h + 1) * LANES]
        for i in range(1, ZH):
            back_copy(1 + m, i, zh, lax.rem(zh + i, ZH)).start()
        target_buffer[aligned(zh, halves)] = in_parts[m, zh]
    for i in range(1, ZH):
        back_copy(0, i, zh, lax.rem(zh + i, ZH)).start()
    act_out[aligned(zh, halves)] = act_part[zh]

    for i in range(1, doms):
        sum_copy(i, lax.rem(dom + doms - i, doms), dom).wait_recv()
    w_got[dom] = w_parts[dom]
    total = w_got[0].astype(F32)
    for d in range(1, doms):
        total = total + w_got[d].astype(F32)
    w_sums[...] = total.reshape(ZH, rows, wide + LANES)

    def zh_copy(i, source, target):
        return remote(
            w_sums.at[target],
            w_zh.at[source],
            sum_s.at[1, i],
            sum_r.at[1, i],
            {"feat": target * near + nr},
        )

    for i in range(1, ZH):
        zh_copy(i, zh, lax.rem(zh + i, ZH)).start()
    w_zh[zh] = w_sums[zh]

    for i in range(1, ZH):
        back_copy(2, i, lax.rem(zh + ZH - i, ZH), zh).wait_recv()
    chain(grad_agg, 0, vals, prev_src)

    for t in range(2 * doms):
        away[t] = runs[links_s[last_src, own_tiles + t]].astype(BF16)

    def return_copy(which, i, source, target):
        pieces = ((away.at[pl.ds(2 * target, 2)], returned), (w_final.at[:, 0:wide], w_all))
        part, buffer = pieces[which]
        return remote(
            part, buffer.at[source], ret_s.at[which, i], ret_r.at[which, i], {"dom": target}
        )

    for i in range(1, doms):
        return_copy(0, i, dom, lax.rem(dom + i, doms)).start()
    for i in range(1, ZH):
        zh_copy(i, lax.rem(zh + ZH - i, ZH), zh).wait_recv()
    total = w_zh[0]
    for h in range(1, ZH):
        total = total + w_zh[h]
    w_final[...] = total
    for i in range(1, doms):
        return_copy(1, i, dom, lax.rem(dom + i, doms)).start()
    returned[dom] = away[pl.ds(2 * dom, 2)]
    w_all[dom] = w_final[:, 0:wide]

    for i in range(1, ZH):
        back_copy(1, i, lax.rem(zh + ZH - i, ZH), zh).wait_recv()
    for t in range(own_tiles):
        total = runs[links_s[last_src, t]]
        if t < dst_tiles:
            total = total + grad_self[t].astype(F32)
        grad_own[t] = total

    for i in range(1, ZH):
        back_copy(0, i, lax.rem(zh + ZH - i, ZH), zh).wait_recv()
    for i in range(1, doms):
        source = lax.rem(dom + doms - i, doms)
        return_copy(0, i, source, dom).wait_recv()
        return_copy(1, i, source, dom).wait_recv()

    for i in range(1, doms):
        target = lax.rem(dom + i, doms)
        halo_copy(i, dom, target).wait_send()
        sum_copy(i, dom, target).wait_send()
        for which in (0, 1):
            share_copy(which, i, dom, target).wait_send()
            return_copy(which, i, dom, target).wait_send()
    for i in range(1, ZH):
        target = lax.rem(zh + i, ZH)
        for which in range(4):
            far_copy(which, i, zh, target).wait_send()
        for which in range(3):
            back_copy(which, i, zh, target).wait_send()
        agg_copy(i, zh, target).wait_send()
        zh_copy(i, zh, target).wait_send()
    for i in range(1, near):
        for which in range(3):
            near_copy(which, i, nr, lax.rem(nr + i, near)).wait_send()

    @pl.when(nr == dom)
    def _():
        for i in range(1, feat_total):
            col_copy(i, lax.rem(feat + i, feat_total)).wait_send()


def finish_kernel(
    doms,
    own_ref,
    returned_ref,
    send_rows,
    hub_rows,
    w_all,
    w_final,
    act_ref,
    act_out,
    feats_out,
    w_self_out,
    w_neigh_out,
    bias_out,
    masked,
):
    own_tiles, rows, _ = own_ref.shape
    dst_tiles = act_ref.shape[0]
    wide = w_all.shape[2]
    hots = []
    for block in range(doms + 1):
        if block == doms:
            index_row = hub_rows[...]
            total = returned_ref[0, 1].astype(F32)
            for d in range(1, doms):
                total = total + returned_ref[d, 1].astype(F32)
            values = total.astype(BF16)
        else:
            index_row = send_rows[block : block + 1, :]
            values = returned_ref[block, 0]
        high = jnp.right_shift(index_row, 7)
        values = values.astype(F32)
        for t in range(own_tiles):
            masked[t, :, block * LANES : (block + 1) * LANES] = jnp.where(
                high == t, values, 0.0
            ).astype(BF16)
        hots.append(column_hot(index_row))
    hot = jnp.concatenate(hots, axis=1)
    added = lax.dot_general(
        masked[...].reshape(own_tiles * rows, (doms + 1) * LANES),
        hot,
        (((1,), (1,)), ((), ())),
        preferred_element_type=F32,
    ).reshape(own_tiles, rows, LANES)
    for t in range(own_tiles):
        feats_out[:, t * LANES : (t + 1) * LANES] = own_ref[t] + added[t]
    for t in range(dst_tiles):
        act_out[:, t * LANES : (t + 1) * LANES] = act_ref[t]
    half = doms // 2
    for d in range(half):
        w_self_out[:, d * wide : (d + 1) * wide] = w_all[d]
        w_neigh_out[:, d * wide : (d + 1) * wide] = w_all[half + d]
    spot = lax.broadcasted_iota(jnp.int32, (rows, LANES), 0)
    lane = lax.broadcasted_iota(jnp.int32, (rows, LANES), 1)
    picked = jnp.where(spot == lane, w_final[:, wide:], 0.0)
    bias_out[...] = jnp.sum(picked, axis=0, keepdims=True)[:, 0:rows]


def shape(dims, dtype):
    return jax.ShapeDtypeStruct(dims, dtype)


def body(
    doms,
    feat_total,
    node_feats,
    send_rows,
    hub_rows,
    tile_dst,
    tile_src,
    tile_count,
    tile_vals,
    w_self,
    w_neigh,
    bias_vec,
    cotangent,
):
    near = feat_total // ZH
    rows, own = node_feats.shape
    own_tiles = own // LANES
    columns = cotangent.shape[1]
    dst_tiles = columns // LANES
    quarter = columns // ZH
    halves = quarter // LANES
    width = w_self.shape[1]
    mine = ZH * rows
    wide = 2 * width // doms
    all_tiles = own_tiles + 2 * doms
    tile_total = tile_src.shape[0]
    key_rows = tile_total // LANES
    dma = pltpu.SemaphoreType.DMA
    in_vmem = pl.BlockSpec(memory_space=pltpu.VMEM)

    send_grid = send_rows.reshape(doms, LANES)
    hub_grid = hub_rows.reshape(1, LANES)

    act_tiles, grad_own, returned, w_all, w_final = pl.pallas_call(
        functools.partial(layer_kernel, doms, near),
        name="layer",
        out_shape=(
            shape((dst_tiles, rows, LANES), BF16),
            shape((own_tiles, rows, LANES), F32),
            shape((doms, 2, rows, LANES), BF16),
            shape((doms, rows, wide), F32),
            shape((rows, wide + LANES), F32),
        ),
        in_specs=[pl.BlockSpec(memory_space=pltpu.SMEM)]
        + [pl.BlockSpec(memory_space=pltpu.HBM)] * 10,
        out_specs=(in_vmem,) * 5,
        scratch_shapes=[
            pltpu.VMEM((rows, own), BF16),
            pltpu.VMEM((doms, LANES), jnp.int32),
            pltpu.VMEM((1, LANES), jnp.int32),
            pltpu.VMEM((key_rows, LANES), jnp.int32),
            pltpu.VMEM((key_rows, LANES), jnp.int32),
            pltpu.VMEM((tile_total, LANES, LANES), BF16),
            pltpu.VMEM((tile_total, LANES, LANES), BF16),
            pltpu.VMEM((tile_total + 1, rows, LANES), F32),
            pltpu.VMEM((4 * key_rows + 8, LANES), jnp.int32),
            pltpu.SMEM((4 * key_rows + 8, LANES), jnp.int32),
            pltpu.VMEM((all_tiles, rows, LANES), BF16),
            pltpu.VMEM((doms, 2, rows, LANES), BF16),
            pltpu.VMEM((2, rows, width), BF16),
            pltpu.VMEM((near, 2, rows, mine), BF16),
            pltpu.VMEM((1, rows), F32),
            pltpu.VMEM((rows, LANES), F32),
            pltpu.VMEM((ZH, rows, LANES), F32),
            pltpu.VMEM((rows, columns), BF16),
            pltpu.VMEM((ZH, rows, quarter), BF16),
            pltpu.VMEM((2, ZH, rows, width), BF16),
            pltpu.VMEM((2, ZH, near, rows, mine), BF16),
            pltpu.VMEM((ZH, near, rows, quarter), BF16),
            pltpu.VMEM((ZH, near, rows, quarter), BF16),
            pltpu.VMEM((rows, columns), BF16),
            pltpu.VMEM((mine, quarter), BF16),
            pltpu.VMEM((ZH, near, rows, quarter), BF16),
            pltpu.VMEM((ZH, halves, rows, LANES), BF16),
            pltpu.VMEM((2, ZH, halves, rows, LANES), BF16),
            pltpu.VMEM((dst_tiles, rows, LANES), BF16),
            pltpu.VMEM((dst_tiles, rows, LANES), BF16),
            pltpu.VMEM((2 * doms, rows, LANES), BF16),
            pltpu.VMEM((doms, mine, wide + LANES), BF16),
            pltpu.VMEM((doms, mine, wide + LANES), BF16),
            pltpu.VMEM((ZH, rows, wide + LANES), F32),
            pltpu.VMEM((ZH, rows, wide + LANES), F32),
            dma((9,)),
            dma((16,)),
            dma,
            dma((doms,)),
            dma((doms,)),
            dma((4, ZH)),
            dma((4, ZH)),
            dma((3, near)),
            dma((3, near)),
            dma((feat_total,)),
            dma((ZH,)),
            dma((2, doms)),
            dma((2, doms)),
            dma((ZH,)),
            dma((ZH,)),
            dma((3, ZH)),
            dma((3, ZH)),
            dma((2, max(doms, ZH))),
            dma((2, max(doms, ZH))),
            dma((2, doms)),
            dma((2, doms)),
        ],
        compiler_params=pltpu.CompilerParams(
            collective_id=0, has_side_effects=True, vmem_limit_bytes=VMEM_LIMIT
        ),
    )(
        tile_count,
        node_feats,
        send_grid,
        hub_grid,
        tile_dst.reshape(key_rows, LANES),
        tile_src.reshape(key_rows, LANES),
        tile_vals,
        w_self,
        w_neigh,
        bias_vec.reshape(1, rows),
        cotangent,
    )

    activations, grad_feats, grad_w_self, grad_w_neigh, grad_bias = pl.pallas_call(
        functools.partial(finish_kernel, doms),
        name="finish",
        out_shape=(
            shape((rows, columns), BF16),
            shape((rows, own), F32),
            shape((rows, width), F32),
            shape((rows, width), F32),
            shape((1, rows), F32),
        ),
        in_specs=[in_vmem] * 7,
        out_specs=(in_vmem,) * 5,
        scratch_shapes=[pltpu.VMEM((own_tiles, rows, (doms + 1) * LANES), BF16)],
        compiler_params=pltpu.CompilerParams(vmem_limit_bytes=VMEM_LIMIT),
    )(grad_own, returned, send_grid, hub_grid, w_all, w_final, act_tiles)
    return (activations, grad_feats, grad_w_self, grad_w_neigh, grad_bias.reshape(rows))


def solution(mesh):
    return jax.shard_map(
        functools.partial(body, mesh.shape["dom"], mesh.shape["feat"]),
        mesh=mesh,
        in_specs=(
            P("feat", "dom"),
            P("dom"),
            P("dom"),
            P("dom"),
            P("dom"),
            P("dom"),
            P("dom", None, None),
            P("feat", None),
            P("feat", None),
            P("feat"),
            P("feat", "dom"),
        ),
        out_specs=(P("feat", "dom"), P("feat", "dom"), P("feat", None), P("feat", None), P("feat")),
        check_vma=False,
    )
```

time: 556 us -> 83.8 us (0.15)
  waiting for transfers between devices: 394 us -> 0 us
  Pallas kernels: 0 us -> 82 us
  matrix products: 49.7 us -> 0 us
  local copies, waits for them, and re-layouts: 34.4 us -> 0 us
  blocking collectives: 26.2 us -> 0 us
  other arithmetic: 19.8 us -> 0 us
  starting transfers between devices: 15.6 us -> 0 us
  between operations: 14.7 us -> 1.29 us
    unnamed x7 -> x0, waiting for transfers between devices: 233 us -> none
    all_gather x2 -> x0, waiting for transfers between devices: 99 us -> none  [the longest x1 76.2 us: body(): lax.all_gather(aggregate, 'feat', axis=0, tiled=True)]
    pallas_call x0 -> x2, Pallas kernels: none -> 82 us  [the longest x1 79 us: body(): pl.pallas_call(functools.partial(layer_kernel, doms, near), name='layer',...]
    psum x1 -> x0, waiting for transfers between devices: 61.9 us -> none  [body(): lax.psum((local_self, local_neigh, local_bias), 'dom')]
    dot_general x10 -> x0, matrix products: 49.7 us -> none  [the longest x1 13 us: body(): jnp.einsum('fkj,kij->fki', picked, tile_vals, preferred_element_type=jnp....]
    unnamed x31 -> x0, local copies, waits for them, and re-layouts: 19.8 us -> none
    all_to_all x2 -> x0, starting transfers between devices: 15.3 us -> none  [the longest x1 8.82 us: body(): lax.all_to_all(halo_grad.astype(jnp.bfloat16), 'dom', split_axis=1, conca...]
    all_gather x1 -> x0, blocking collectives: 13.5 us -> none  [body(): lax.all_gather(jnp.take(node_feats, hub_rows, axis=1), 'dom', axis=1, til...]
  transfers between devices with their start and end apart: 7 -> 0, of which waited for: 5 -> 0; matrix products, arithmetic and copies ran while one was open for 10% -> 0% of each run, Pallas kernels for 0% -> 0%
where the time goes in v2:
time: 83.8 us; the launch traced here: 83.2 us
  Pallas kernels  82 us (98%)
  between operations  1.29 us (2%)
    pallas_call x1, Pallas kernels, body(): pl.pallas_call(functools.partial(layer_kernel, doms, near), name='layer',...  79 us
    pallas_call x1, Pallas kernels, body(): pl.pallas_call(functools.partial(finish_kernel, doms), name='finish', out...  2.91 us

profile of v2, /device:TPU:1, one launch (start us, length us, event | category | flops | bytes accessed | tf_op | source)
XLA Modules:
  0.0 83.2 jit_solution(7211966755928694503)
XLA Ops:
  1.3 79.0 %layer.1 = (bf16[8,32,128]{2,1,0:T(8,128)(2,1)}, f32[32,32,128]{2,1,0:T(8,128)}, bf16[8,2,32,128]{3,2,1,0:T(8,128)(2,1)}, f32[8,32,256]{2,1,0:T(8,128)}, f32[32,384]{1,0:T(8,128)}) custom-call(s32[1]{0:T(128)S(6)} %copy.16.count_ref, bf16[32,4096]{1,0:T(8,128)(2,1)} %feats_hbm.1, s32[8,128]{1,0:T(8,128)} %bitcast.6, s32[1,128]{1,0:T(1,128)} %bitcast.8, ...), custom_call_target="tpu_custom_call" | custom-call | tf_op jit(solution)/shard_map/layer/pallas_call | solution.py:722
  80.3 2.9 %finish.1 = (bf16[32,1024]{1,0:T(8,128)(2,1)}, f32[32,4096]{1,0:T(8,128)}, f32[32,1024]{1,0:T(8,128)}, f32[32,1024]{1,0:T(8,128)}, f32[1,32]{1,0:T(1,128)}) custom-call(f32[32,32,128]{2,1,0:T(8,128)} %get-tuple-element.15.own_ref, bf16[8,2,32,128]{3,2,1,0:T(8,128)(2,1)} %get-tuple-element.16.returned_ref, s32[8,128]{1,0:T(8,128)} %bitcast.7, ...), custom_call_target="tpu_custom_call" | custom-call | tf_op jit(solution)/shard_map/finish/pallas_call | solution.py:810

commit v3 on v2

--- a/solution.py
+++ b/solution.py
@@ -13,7 +13,8 @@
 ZH = 4
 LANES = 128
 VMEM_LIMIT = 60 * 1024 * 1024
-SUB = 64
+SUB = 128
+SUBLANES = 8
 
 
 def remote(src, dst, send_sem, recv_sem, where):
@@ -101,6 +102,7 @@
     picked,
     w_both,
     w_regrouped,
+    w_columns,
     bias,
     bias_wide,
     bias_part,
@@ -133,6 +135,7 @@
     near_r,
     col_s,
     col_r,
+    col_near_r,
     share_s,
     share_r,
     agg_s,
@@ -156,7 +159,6 @@
     wide = 2 * width // doms
     tile_total = vals.shape[0]
     key_rows = tile_total // LANES
-    feat_total = ZH * near
     dom, feat, zh, nr = place(near)
 
     barrier = pltpu.get_barrier_semaphore()
@@ -178,16 +180,6 @@
             device_id={"feat": zh * near + lax.rem(nr + i, near)},
             device_id_type=MESH,
         )
-
-    @pl.when(nr != dom)
-    def _():
-        for i in range(1, ZH):
-            pl.semaphore_signal(
-                barrier,
-                inc=1,
-                device_id={"feat": lax.rem(zh + i, ZH) * near + dom},
-                device_id_type=MESH,
-            )
 
     loads = [
         pltpu.make_async_copy(source, target, load_sem.at[i])
@@ -240,54 +232,6 @@
             for d in range(doms):
                 picked[d, 1] = total
 
-    common = (doms - 1) + (ZH - 1) + (near - 1)
-
-    @pl.when(nr == dom)
-    def _():
-        pl.semaphore_wait(barrier, common + (ZH - 1) * (near - 1))
-
-    @pl.when(nr != dom)
-    def _():
-        pl.semaphore_wait(barrier, common)
-
-    def halo_copy(i, source, target):
-        return remote(
-            picked.at[target],
-            table.at[pl.ds(own_tiles + 2 * source, 2)],
-            halo_s.at[i],
-            halo_r.at[i],
-            {"dom": target},
-        )
-
-    for i in range(1, doms):
-        halo_copy(i, dom, lax.rem(dom + i, doms)).start()
-
-    def far_copy(which, i, source, target):
-        sources = (
-            feats.at[:, aligned(target, quarter)],
-            w_both.at[:, :, aligned(dom, chunk)],
-            cot.at[:, aligned(target, quarter)],
-            bias_wide,
-        )
-        targets = (
-            x_self.at[source, nr],
-            wrow.at[:, source, :, aligned(dom, chunk)],
-            cot_part.at[source],
-            bias_part.at[source],
-        )
-        return remote(
-            sources[which],
-            targets[which],
-            far_s.at[which, i],
-            far_r.at[which, i],
-            {"feat": target * near + nr},
-        )
-
-    for i in range(1, ZH):
-        far_copy(0, i, zh, lax.rem(zh + i, ZH)).start()
-    for i in range(1, ZH):
-        far_copy(1, i, zh, lax.rem(zh + i, ZH)).start()
-
     lanes_at = lax.broadcasted_iota(jnp.int32, (rows, LANES), 1)
     for m in range(2):
         for n in range(near):
@@ -301,36 +245,22 @@
                     piece = pltpu.roll(piece, shift, 1)
                 inside = (lanes_at >= h * rows) & (lanes_at < (h + 1) * rows)
                 joined = jnp.where(inside, piece, joined)
-            w_regrouped[n, m] = joined.astype(BF16)
-
-    def col_copy(i, target):
-        return remote(
-            w_regrouped.at[lax.rem(target, near)],
-            wcol.at[:, zh, nr],
-            col_s.at[i],
-            col_r.at[zh],
-            {"feat": target},
-        )
-
-    @pl.when(nr == dom)
-    def _():
-        for i in range(1, feat_total):
-            col_copy(i, lax.rem(feat + i, feat_total)).start()
-        wcol[:, zh, nr] = w_regrouped[nr]
+            w_regrouped[m, n] = joined.astype(BF16)
 
     spot = lax.broadcasted_iota(jnp.int32, (rows, rows), 0)
     lane = lax.broadcasted_iota(jnp.int32, (rows, rows), 1)
     bias_column = jnp.sum(jnp.where(spot == lane, bias[...], 0.0), axis=1, keepdims=True)
     bias_wide[...] = jnp.broadcast_to(bias_column, (rows, LANES))
-    for which in (2, 3):
-        for i in range(1, ZH):
-            far_copy(which, i, zh, lax.rem(zh + i, ZH)).start()
-
     x_self[zh, nr] = feats[:, aligned(zh, quarter)]
     wrow[:, zh, :, aligned(dom, chunk)] = w_both[:, :, aligned(dom, chunk)]
     cot_part[zh] = cot[:, aligned(zh, quarter)]
     bias_part[zh] = bias_wide[...]
     table[pl.ds(own_tiles + 2 * dom, 2)] = picked[dom]
+
+
+    @pl.when(nr == dom)
+    def _():
+        w_columns[:, zh] = w_regrouped[...]
 
     given = src[...]
     outside = given - own_tiles
@@ -346,24 +276,82 @@
     link_copy = pltpu.make_async_copy(links, links_s, link_sem)
     link_copy.start()
 
-    def flip(b):
+    pl.semaphore_wait(barrier, (doms - 1) + (ZH - 1) + (near - 1))
+
+    def halo_copy(i, source, target):
+        return remote(
+            picked.at[target],
+            table.at[pl.ds(own_tiles + 2 * source, 2)],
+            halo_s.at[i],
+            halo_r.at[i],
+            {"dom": target},
+        )
+
+    for i in range(1, doms):
+        halo_copy(i, dom, lax.rem(dom + i, doms)).start()
+
+    def far_copy(which, i, source, target):
+        sources = (
+            feats.at[:, aligned(target, quarter)],
+            w_both.at[:, :, aligned(dom, chunk)],
+            cot.at[:, aligned(target, quarter)],
+            bias_wide,
+        )
+        targets = (
+            x_self.at[source, nr],
+            wrow.at[:, source, :, aligned(dom, chunk)],
+            cot_part.at[source],
+            bias_part.at[source],
+        )
+        return remote(
+            sources[which],
+            targets[which],
+            far_s.at[which, i],
+            far_r.at[which, i],
+            {"feat": target * near + nr},
+        )
+
+    for i in range(1, ZH):
+        far_copy(0, i, zh, lax.rem(zh + i, ZH)).start()
+    for i in range(1, ZH):
+        far_copy(1, i, zh, lax.rem(zh + i, ZH)).start()
+
+    def col_far_copy(i, source, target):
+        return remote(
+            w_regrouped,
+            w_columns.at[:, source],
+            col_s.at[0, i],
+            col_r.at[i],
+            {"feat": target * near + nr},
+        )
+
+    def col_near_copy(i, target):
+        return remote(
+            w_columns.at[:, :, target],
+            wcol.at[:, :, dom],
+            col_s.at[1, i],
+            col_near_r,
+            {"feat": zh * near + target},
+        )
+
+    @pl.when(nr == dom)
+    def _():
+        for i in range(1, ZH):
+            col_far_copy(i, zh, lax.rem(zh + i, ZH)).start()
+
+    for which in (2, 3):
+        for i in range(1, ZH):
+            far_copy(which, i, zh, lax.rem(zh + i, ZH)).start()
+
+
+    for b in range(blocks):
         vals_loads[b].wait()
 
-        def some(j, carry):
-            for t in range(8):
-                k = b * block + j * 8 + t
-                flipped[k] = jnp.transpose(vals[k])
+        def flip(k, carry):
+            flipped[k] = jnp.transpose(vals[k])
             return carry
 
-        lax.fori_loop(0, block // 8, some, 0)
-
-    early = blocks // 4
-    for b in range(early):
-        flip(b)
-
-    for which in (0, 1):
-        for i in range(1, ZH):
-            far_copy(which, i, lax.rem(zh + ZH - i, ZH), zh).wait_recv()
+        lax.fori_loop(b * block, (b + 1) * block, flip, 0, unroll=True)
 
     def near_copy(which, i, source, target):
         buffer = (x_self, x_agg, g_all)[which]
@@ -375,38 +363,35 @@
             {"feat": zh * near + target},
         )
 
+    for i in range(1, ZH):
+        far_copy(0, i, lax.rem(zh + ZH - i, ZH), zh).wait_recv()
     for i in range(1, near):
         near_copy(0, i, nr, lax.rem(nr + i, near)).start()
 
-    for h in range(ZH):
-
-        @pl.when((nr != dom) | (zh != h))
-        def _():
-            remote(
-                w_regrouped.at[0],
-                wcol.at[:, h, dom],
-                col_s.at[0],
-                col_r.at[h],
-                {"feat": feat},
-            ).wait_recv()
+    @pl.when(nr == dom)
+    def _():
+        for i in range(1, ZH):
+            col_far_copy(i, lax.rem(zh + ZH - i, ZH), zh).wait_recv()
+        for i in range(1, near):
+            col_near_copy(i, lax.rem(nr + i, near)).start()
+        wcol[:, :, dom] = w_columns[:, :, nr]
 
     def share_copy(which, i, source, target):
         part = wcol.at[:, :, source] if which else wrow.at[:, :, :, aligned(source, chunk)]
         return remote(part, part, share_s.at[which, i], share_r.at[which, i], {"dom": target})
 
-    for which in (0, 1):
-        for i in range(1, doms):
-            share_copy(which, i, dom, lax.rem(dom + i, doms)).start()
-
-    for b in range(early, blocks):
-        flip(b)
+    for i in range(1, ZH):
+        far_copy(1, i, lax.rem(zh + ZH - i, ZH), zh).wait_recv()
+    for i in range(1, doms):
+        share_copy(0, i, dom, lax.rem(dom + i, doms)).start()
+
     link_copy.wait()
     for i in range(1, doms):
         halo_copy(i, lax.rem(dom + doms - i, doms), dom).wait_recv()
 
     runs[tile_total] = jnp.zeros((rows, LANES), F32)
 
-    def chain(left, left_row, tiles, prev_row):
+    def chain(left, left_row, tiles, prev_row, first, last):
         def some(j, carry):
             row = lax.div(j * SUB, LANES)
             start = lax.rem(j * SUB, LANES)
@@ -419,9 +404,10 @@
                 runs[j * SUB + t] = runs[links_s[prev_row + row, start + t]] + product
             return carry
 
-        lax.fori_loop(0, tile_total // SUB, some, 0)
-
-    chain(table, key_rows, flipped, prev_dst)
+        lax.fori_loop(first, last, some, 0)
+
+    steps = tile_total // SUB
+    chain(table, key_rows, flipped, prev_dst, 0, steps)
     for u in range(dst_tiles):
         agg[:, u * LANES : (u + 1) * LANES] = runs[links_s[last_dst, u]].astype(BF16)
 
@@ -437,6 +423,13 @@
     for i in range(1, ZH):
         agg_copy(i, zh, lax.rem(zh + i, ZH)).start()
     x_agg[zh, nr] = agg[:, aligned(zh, quarter)]
+
+    @pl.when(nr != dom)
+    def _():
+        col_near_copy(0, nr).wait_recv()
+
+    for i in range(1, doms):
+        share_copy(1, i, dom, lax.rem(dom + i, doms)).start()
     for i in range(1, near):
         near_copy(0, i, lax.rem(nr + near - i, near), nr).wait_recv()
     for i in range(1, doms):
@@ -487,8 +480,9 @@
 
     over_x = (((1,), (1,)), ((), ()))
     half_doms = doms // 2
-    bias_sum = jnp.sum(grad.astype(F32), axis=1, keepdims=True)
-    bias_sum = jnp.broadcast_to(bias_sum, (mine, LANES)).astype(BF16)
+    ones = jnp.ones((2 * SUBLANES, quarter), BF16)
+    bias_sum = lax.dot_general(ones, g_part[...], over_x, preferred_element_type=F32)
+    bias_sum = bias_sum.astype(BF16)
     for m, x_ref in enumerate((x_self, x_agg)):
         product = lax.dot_general(
             g_part[...],
@@ -497,9 +491,10 @@
             preferred_element_type=F32,
         ).astype(BF16)
         for d in range(half_doms):
-            w_parts[m * half_doms + d, :, 0:wide] = product[:, d * wide : (d + 1) * wide]
+            w_parts[m * half_doms + d, 0:mine] = product[:, d * wide : (d + 1) * wide]
     for d in range(doms):
-        w_parts[d, :, wide:] = bias_sum
+        w_parts[d, mine:, 0:mine] = bias_sum
+        w_parts[d, mine:, mine:] = jnp.zeros((2 * SUBLANES, wide - mine), BF16)
 
     def sum_copy(i, source, target):
         return remote(
@@ -541,7 +536,9 @@
     total = w_got[0].astype(F32)
     for d in range(1, doms):
         total = total + w_got[d].astype(F32)
-    w_sums[...] = total.reshape(ZH, rows, wide + LANES)
+    w_sums[:, 0:rows] = total[0:mine].reshape(ZH, rows, wide)
+    for h in range(ZH):
+        w_sums[h, rows:] = total[mine : mine + SUBLANES]
 
     def zh_copy(i, source, target):
         return remote(
@@ -558,11 +555,6 @@
 
     for i in range(1, ZH):
         back_copy(2, i, lax.rem(zh + ZH - i, ZH), zh).wait_recv()
-    chain(grad_agg, 0, vals, prev_src)
-
-    for t in range(2 * doms):
-        away[t] = runs[links_s[last_src, own_tiles + t]].astype(BF16)
-
     def return_copy(which, i, source, target):
         pieces = ((away.at[pl.ds(2 * target, 2)], returned), (w_final.at[:, 0:wide], w_all))
         part, buffer = pieces[which]
@@ -570,16 +562,28 @@
             part, buffer.at[source], ret_s.at[which, i], ret_r.at[which, i], {"dom": target}
         )
 
-    for i in range(1, doms):
-        return_copy(0, i, dom, lax.rem(dom + i, doms)).start()
+    chain(grad_agg, 0, vals, prev_src, 0, steps // 2)
+
     for i in range(1, ZH):
         zh_copy(i, lax.rem(zh + ZH - i, ZH), zh).wait_recv()
     total = w_zh[0]
     for h in range(1, ZH):
         total = total + w_zh[h]
-    w_final[...] = total
+    spot = lax.broadcasted_iota(jnp.int32, (rows, mine), 0) + zh * rows
+    lane = lax.broadcasted_iota(jnp.int32, (rows, mine), 1)
+    bias_row = total[rows : rows + 1, 0:mine]
+    bias_column = jnp.sum(jnp.where(spot == lane, bias_row, 0.0), axis=1, keepdims=True)
+    w_final[:, 0:wide] = total[0:rows]
+    w_final[:, wide:] = jnp.broadcast_to(bias_column, (rows, LANES))
     for i in range(1, doms):
         return_copy(1, i, dom, lax.rem(dom + i, doms)).start()
+    chain(grad_agg, 0, vals, prev_src, steps // 2, steps)
+
+    for t in range(2 * doms):
+        away[t] = runs[links_s[last_src, own_tiles + t]].astype(BF16)
+
+    for i in range(1, doms):
+        return_copy(0, i, dom, lax.rem(dom + i, doms)).start()
     returned[dom] = away[pl.ds(2 * dom, 2)]
     w_all[dom] = w_final[:, 0:wide]
 
@@ -619,8 +623,10 @@
 
     @pl.when(nr == dom)
     def _():
-        for i in range(1, feat_total):
-            col_copy(i, lax.rem(feat + i, feat_total)).wait_send()
+        for i in range(1, ZH):
+            col_far_copy(i, zh, lax.rem(zh + i, ZH)).wait_send()
+        for i in range(1, near):
+            col_near_copy(i, lax.rem(nr + i, near)).wait_send()
 
 
 def finish_kernel(
@@ -746,7 +752,8 @@
             pltpu.VMEM((all_tiles, rows, LANES), BF16),
             pltpu.VMEM((doms, 2, rows, LANES), BF16),
             pltpu.VMEM((2, rows, width), BF16),
-            pltpu.VMEM((near, 2, rows, mine), BF16),
+            pltpu.VMEM((2, near, rows, mine), BF16),
+            pltpu.VMEM((2, ZH, near, rows, mine), BF16),
             pltpu.VMEM((1, rows), F32),
             pltpu.VMEM((rows, LANES), F32),
             pltpu.VMEM((ZH, rows, LANES), F32),
@@ -764,10 +771,10 @@
             pltpu.VMEM((dst_tiles, rows, LANES), BF16),
             pltpu.VMEM((dst_tiles, rows, LANES), BF16),
             pltpu.VMEM((2 * doms, rows, LANES), BF16),
-            pltpu.VMEM((doms, mine, wide + LANES), BF16),
-            pltpu.VMEM((doms, mine, wide + LANES), BF16),
-            pltpu.VMEM((ZH, rows, wide + LANES), F32),
-            pltpu.VMEM((ZH, rows, wide + LANES), F32),
+            pltpu.VMEM((doms, mine + 2 * SUBLANES, wide), BF16),
+            pltpu.VMEM((doms, mine + 2 * SUBLANES, wide), BF16),
+            pltpu.VMEM((ZH, rows + SUBLANES, wide), F32),
+            pltpu.VMEM((ZH, rows + SUBLANES, wide), F32),
             dma((9,)),
             dma((16,)),
             dma,
@@ -777,8 +784,9 @@
             dma((4, ZH)),
             dma((3, near)),
             dma((3, near)),
-            dma((feat_total,)),
+            dma((2, max(near, ZH))),
             dma((ZH,)),
+            dma,
             dma((2, doms)),
             dma((2, doms)),
             dma((ZH,)),

time: 83.8 us -> 75.5 us (0.901)
  Pallas kernels: 82 us -> 73.8 us
    pallas_call x1, Pallas kernels: 79 us -> 70.9 us  [body(): pl.pallas_call(functools.partial(layer_kernel, doms, near), name='layer',...]
where the time goes in v3:
time: 75.5 us; the launch traced here: 75.1 us
  Pallas kernels  73.8 us (98%)
  between operations  1.29 us (2%)
    pallas_call x1, Pallas kernels, body(): pl.pallas_call(functools.partial(layer_kernel, doms, near), name='layer',...  70.9 us
    pallas_call x1, Pallas kernels, body(): pl.pallas_call(functools.partial(finish_kernel, doms), name='finish', out...  2.91 us

profile of v3, /device:TPU:1, one launch (start us, length us, event | category | flops | bytes accessed | tf_op | source)
XLA Modules:
  0.0 75.1 jit_solution(14517424805433543226)
XLA Ops:
  1.3 70.9 %layer.1 = (bf16[8,32,128]{2,1,0:T(8,128)(2,1)}, f32[32,32,128]{2,1,0:T(8,128)}, bf16[8,2,32,128]{3,2,1,0:T(8,128)(2,1)}, f32[8,32,256]{2,1,0:T(8,128)}, f32[32,384]{1,0:T(8,128)}) custom-call(s32[1]{0:T(128)S(6)} %copy.16.count_ref, bf16[32,4096]{1,0:T(8,128)(2,1)} %feats_hbm.1, s32[8,128]{1,0:T(8,128)} %bitcast.6, s32[1,128]{1,0:T(1,128)} %bitcast.8, ...), custom_call_target="tpu_custom_call" | custom-call | tf_op jit(solution)/shard_map/layer/pallas_call | solution.py:728
  72.2 2.9 %finish.1 = (bf16[32,1024]{1,0:T(8,128)(2,1)}, f32[32,4096]{1,0:T(8,128)}, f32[32,1024]{1,0:T(8,128)}, f32[32,1024]{1,0:T(8,128)}, f32[1,32]{1,0:T(1,128)}) custom-call(f32[32,32,128]{2,1,0:T(8,128)} %get-tuple-element.15.own_ref, bf16[8,2,32,128]{3,2,1,0:T(8,128)(2,1)} %get-tuple-element.16.returned_ref, s32[8,128]{1,0:T(8,128)} %bitcast.7, ...), custom_call_target="tpu_custom_call" | custom-call | tf_op jit(solution)/shard_map/finish/pallas_call | solution.py:818

commit v4 on v3

--- a/solution.py
+++ b/solution.py
@@ -161,26 +161,6 @@
     key_rows = tile_total // LANES
     dom, feat, zh, nr = place(near)
 
-    barrier = pltpu.get_barrier_semaphore()
-    for i in range(1, doms):
-        pl.semaphore_signal(
-            barrier, inc=1, device_id={"dom": lax.rem(dom + i, doms)}, device_id_type=MESH
-        )
-    for i in range(1, ZH):
-        pl.semaphore_signal(
-            barrier,
-            inc=1,
-            device_id={"feat": lax.rem(zh + i, ZH) * near + nr},
-            device_id_type=MESH,
-        )
-    for i in range(1, near):
-        pl.semaphore_signal(
-            barrier,
-            inc=1,
-            device_id={"feat": zh * near + lax.rem(nr + i, near)},
-            device_id_type=MESH,
-        )
-
     loads = [
         pltpu.make_async_copy(source, target, load_sem.at[i])
         for i, (source, target) in enumerate(
@@ -211,6 +191,27 @@
     ]
     for load in vals_loads:
         load.start()
+
+    barrier = pltpu.get_barrier_semaphore()
+    for i in range(1, doms):
+        pl.semaphore_signal(
+            barrier, inc=1, device_id={"dom": lax.rem(dom + i, doms)}, device_id_type=MESH
+        )
+    for i in range(1, ZH):
+        pl.semaphore_signal(
+            barrier,
+            inc=1,
+            device_id={"feat": lax.rem(zh + i, ZH) * near + nr},
+            device_id_type=MESH,
+        )
+    for i in range(1, near):
+        pl.semaphore_signal(
+            barrier,
+            inc=1,
+            device_id={"feat": zh * near + lax.rem(nr + i, near)},
+            device_id_type=MESH,
+        )
+
     for load in loads:
         load.wait()
 
@@ -339,10 +340,6 @@
         for i in range(1, ZH):
             col_far_copy(i, zh, lax.rem(zh + i, ZH)).start()
 
-    for which in (2, 3):
-        for i in range(1, ZH):
-            far_copy(which, i, zh, lax.rem(zh + i, ZH)).start()
-
 
     for b in range(blocks):
         vals_loads[b].wait()
@@ -362,28 +359,6 @@
             near_r.at[which, i],
             {"feat": zh * near + target},
         )
-
-    for i in range(1, ZH):
-        far_copy(0, i, lax.rem(zh + ZH - i, ZH), zh).wait_recv()
-    for i in range(1, near):
-        near_copy(0, i, nr, lax.rem(nr + i, near)).start()
-
-    @pl.when(nr == dom)
-    def _():
-        for i in range(1, ZH):
-            col_far_copy(i, lax.rem(zh + ZH - i, ZH), zh).wait_recv()
-        for i in range(1, near):
-            col_near_copy(i, lax.rem(nr + i, near)).start()
-        wcol[:, :, dom] = w_columns[:, :, nr]
-
-    def share_copy(which, i, source, target):
-        part = wcol.at[:, :, source] if which else wrow.at[:, :, :, aligned(source, chunk)]
-        return remote(part, part, share_s.at[which, i], share_r.at[which, i], {"dom": target})
-
-    for i in range(1, ZH):
-        far_copy(1, i, lax.rem(zh + ZH - i, ZH), zh).wait_recv()
-    for i in range(1, doms):
-        share_copy(0, i, dom, lax.rem(dom + i, doms)).start()
 
     link_copy.wait()
     for i in range(1, doms):
@@ -424,6 +399,37 @@
         agg_copy(i, zh, lax.rem(zh + i, ZH)).start()
     x_agg[zh, nr] = agg[:, aligned(zh, quarter)]
 
+    def share_copy(which, i, source, target):
+        part = wcol.at[:, :, source] if which else wrow.at[:, :, :, aligned(source, chunk)]
+        return remote(part, part, share_s.at[which, i], share_r.at[which, i], {"dom": target})
+
+    for i in range(1, ZH):
+        far_copy(0, i, lax.rem(zh + ZH - i, ZH), zh).wait_recv()
+    for i in range(1, near):
+        near_copy(0, i, nr, lax.rem(nr + i, near)).start()
+
+    @pl.when(nr == dom)
+    def _():
+        for i in range(1, ZH):
+            col_far_copy(i, lax.rem(zh + ZH - i, ZH), zh).wait_recv()
+        for i in range(1, near):
+            col_near_copy(i, lax.rem(nr + i, near)).start()
+        wcol[:, :, dom] = w_columns[:, :, nr]
+
+    for i in range(1, ZH):
+        far_copy(1, i, lax.rem(zh + ZH - i, ZH), zh).wait_recv()
+    for i in range(1, doms):
+        share_copy(0, i, dom, lax.rem(dom + i, doms)).start()
+
+    for which in (2, 3):
+        for i in range(1, ZH):
+            far_copy(which, i, zh, lax.rem(zh + i, ZH)).start()
+
+    for i in range(1, ZH):
+        agg_copy(i, lax.rem(zh + ZH - i, ZH), zh).wait_recv()
+    for i in range(1, near):
+        near_copy(1, i, nr, lax.rem(nr + i, near)).start()
+
     @pl.when(nr != dom)
     def _():
         col_near_copy(0, nr).wait_recv()
@@ -439,10 +445,6 @@
         x_self[...].reshape(width, quarter),
         preferred_element_type=F32,
     )
-    for i in range(1, ZH):
-        agg_copy(i, lax.rem(zh + ZH - i, ZH), zh).wait_recv()
-    for i in range(1, near):
-        near_copy(1, i, nr, lax.rem(nr + i, near)).start()
     for which in (2, 3):
         for i in range(1, ZH):
             far_copy(which, i, lax.rem(zh + ZH - i, ZH), zh).wait_recv()
@@ -598,17 +600,11 @@
     for i in range(1, ZH):
         back_copy(0, i, lax.rem(zh + ZH - i, ZH), zh).wait_recv()
     for i in range(1, doms):
-        source = lax.rem(dom + doms - i, doms)
-        return_copy(0, i, source, dom).wait_recv()
-        return_copy(1, i, source, dom).wait_recv()
-
-    for i in range(1, doms):
         target = lax.rem(dom + i, doms)
         halo_copy(i, dom, target).wait_send()
         sum_copy(i, dom, target).wait_send()
         for which in (0, 1):
             share_copy(which, i, dom, target).wait_send()
-            return_copy(which, i, dom, target).wait_send()
     for i in range(1, ZH):
         target = lax.rem(zh + i, ZH)
         for which in range(4):
@@ -627,6 +623,12 @@
             col_far_copy(i, zh, lax.rem(zh + i, ZH)).wait_send()
         for i in range(1, near):
             col_near_copy(i, lax.rem(nr + i, near)).wait_send()
+
+    for i in range(1, doms):
+        source = lax.rem(dom + doms - i, doms)
+        for which in (0, 1):
+            return_copy(which, i, source, dom).wait_recv()
+            return_copy(which, i, dom, lax.rem(dom + i, doms)).wait_send()
 
 
 def finish_kernel(

time: 75.5 us -> 77.5 us (1.026)
  Pallas kernels: 73.8 us -> 76.1 us
    pallas_call x1, Pallas kernels: 70.9 us -> 73.2 us  [body(): pl.pallas_call(functools.partial(layer_kernel, doms, near), name='layer',...]
where the time goes in v4:
time: 77.5 us; the launch traced here: 77.4 us
  Pallas kernels  76.1 us (98%)
  between operations  1.29 us (2%)
    pallas_call x1, Pallas kernels, body(): pl.pallas_call(functools.partial(layer_kernel, doms, near), name='layer',...  73.2 us
    pallas_call x1, Pallas kernels, body(): pl.pallas_call(functools.partial(finish_kernel, doms), name='finish', out...  2.92 us

profile of v4, /device:TPU:1, one launch (start us, length us, event | category | flops | bytes accessed | tf_op | source)
XLA Modules:
  0.0 77.4 jit_solution(10378633185987955386)
XLA Ops:
  1.3 73.2 %layer.1 = (bf16[8,32,128]{2,1,0:T(8,128)(2,1)}, f32[32,32,128]{2,1,0:T(8,128)}, bf16[8,2,32,128]{3,2,1,0:T(8,128)(2,1)}, f32[8,32,256]{2,1,0:T(8,128)}, f32[32,384]{1,0:T(8,128)}) custom-call(s32[1]{0:T(128)S(6)} %copy.16.count_ref, bf16[32,4096]{1,0:T(8,128)(2,1)} %feats_hbm.1, s32[8,128]{1,0:T(8,128)} %bitcast.6, s32[1,128]{1,0:T(1,128)} %bitcast.8, ...), custom_call_target="tpu_custom_call" | custom-call | tf_op jit(solution)/shard_map/layer/pallas_call | solution.py:730
  74.5 2.9 %finish.1 = (bf16[32,1024]{1,0:T(8,128)(2,1)}, f32[32,4096]{1,0:T(8,128)}, f32[32,1024]{1,0:T(8,128)}, f32[32,1024]{1,0:T(8,128)}, f32[1,32]{1,0:T(1,128)}) custom-call(f32[32,32,128]{2,1,0:T(8,128)} %get-tuple-element.15.own_ref, bf16[8,2,32,128]{3,2,1,0:T(8,128)(2,1)} %get-tuple-element.16.returned_ref, s32[8,128]{1,0:T(8,128)} %bitcast.7, ...), custom_call_target="tpu_custom_call" | custom-call | tf_op jit(solution)/shard_map/finish/pallas_call | solution.py:820

commit v5 on v4

--- a/solution.py
+++ b/solution.py
@@ -12,7 +12,7 @@
 BF16 = jnp.bfloat16
 ZH = 4
 LANES = 128
-VMEM_LIMIT = 60 * 1024 * 1024
+VMEM_LIMIT = 52 * 1024 * 1024
 SUB = 128
 SUBLANES = 8
 
@@ -360,6 +360,10 @@
             {"feat": zh * near + target},
         )
 
+    for i in range(1, ZH):
+        far_copy(0, i, lax.rem(zh + ZH - i, ZH), zh).wait_recv()
+    for i in range(1, near):
+        near_copy(0, i, nr, lax.rem(nr + i, near)).start()
     link_copy.wait()
     for i in range(1, doms):
         halo_copy(i, lax.rem(dom + doms - i, doms), dom).wait_recv()
@@ -403,10 +407,6 @@
         part = wcol.at[:, :, source] if which else wrow.at[:, :, :, aligned(source, chunk)]
         return remote(part, part, share_s.at[which, i], share_r.at[which, i], {"dom": target})
 
-    for i in range(1, ZH):
-        far_copy(0, i, lax.rem(zh + ZH - i, ZH), zh).wait_recv()
-    for i in range(1, near):
-        near_copy(0, i, nr, lax.rem(nr + i, near)).start()
 
     @pl.when(nr == dom)
     def _():
@@ -805,16 +805,21 @@
         ),
     )(
         tile_count,
-        node_feats,
-        send_grid,
-        hub_grid,
-        tile_dst.reshape(key_rows, LANES),
-        tile_src.reshape(key_rows, LANES),
-        tile_vals,
-        w_self,
-        w_neigh,
-        bias_vec.reshape(1, rows),
-        cotangent,
+        *[
+            pltpu.with_memory_space_constraint(array, pltpu.HBM)
+            for array in (
+                node_feats,
+                send_grid,
+                hub_grid,
+                tile_dst.reshape(key_rows, LANES),
+                tile_src.reshape(key_rows, LANES),
+                tile_vals,
+                w_self,
+                w_neigh,
+                bias_vec.reshape(1, rows),
+                cotangent,
+            )
+        ],
     )
 
     activations, grad_feats, grad_w_self, grad_w_neigh, grad_bias = pl.pallas_call(

time: 77.5 us -> 72.2 us (0.932); the launches traced: 77.4 us -> 70.8 us
  Pallas kernels: 76.1 us -> 69.5 us
    pallas_call x1, Pallas kernels: 73.2 us -> 67.8 us  [body(): pl.pallas_call(functools.partial(layer_kernel, doms, near), name='layer',...]
    pallas_call x1, Pallas kernels: 2.92 us -> 1.68 us  [body(): pl.pallas_call(functools.partial(finish_kernel, doms), name='finish', out...]
where the time goes in v5:
time: 72.2 us; the launch traced here: 70.8 us
  Pallas kernels  69.5 us (96%)
  between operations  1.34 us (2%)
    pallas_call x1, Pallas kernels, body(): pl.pallas_call(functools.partial(layer_kernel, doms, near), name='layer',...  67.8 us
    pallas_call x1, Pallas kernels, body(): pl.pallas_call(functools.partial(finish_kernel, doms), name='finish', out...  1.68 us

profile of v5, /device:TPU:1, one launch (start us, length us, event | category | flops | bytes accessed | tf_op | source)
XLA Modules:
  0.0 70.8 jit_solution(10725359269726160846)
XLA Ops:
  0.6 0.0 copy-start.1
  0.6 0.0 copy-start
  1.3 67.8 %layer.1 = (bf16[8,32,128]{2,1,0:T(8,128)(2,1)S(1)}, f32[32,32,128]{2,1,0:T(8,128)S(1)}, bf16[8,2,32,128]{3,2,1,0:T(8,128)(2,1)S(1)}, f32[8,32,256]{2,1,0:T(8,128)S(1)}, f32[32,384]{1,0:T(8,128)S(1)}) custom-call(s32[1]{0:T(128)S(6)} %copy.16.count_ref, bf16[32,4096]{1,0:T(8,128)(2,1)} %feats_hbm.1, s32[8,128]{1,0:T(8,128)} %bitcast.6, s32[1,128]{1,0:T(1,128)} %bitcast.8, ...), custom_call_target="tpu_custom_call" | custom-call | tf_op jit(solution)/shard_map/layer/pallas_call | solution.py:730
  69.1 0.0 copy-done.1
  69.1 0.0 copy-done
  69.2 1.7 %finish.1 = (bf16[32,1024]{1,0:T(8,128)(2,1)}, f32[32,4096]{1,0:T(8,128)}, f32[32,1024]{1,0:T(8,128)}, f32[32,1024]{1,0:T(8,128)}, f32[1,32]{1,0:T(1,128)}) custom-call(f32[32,32,128]{2,1,0:T(8,128)S(1)} %get-tuple-element.15.own_ref, bf16[8,2,32,128]{3,2,1,0:T(8,128)(2,1)S(1)} %get-tuple-element.16.returned_ref, s32[8,128]{1,0:T(8,128)S(1)} %bitcast.7, ...), custom_call_target="tpu_custom_call" | custom-call | tf_op jit(solution)/shard_map/finish/pallas_call | solution.py:825
Async XLA Ops:
  0.6 68.5 %copy-start.1 = (s32[128]{0:T(128)S(1)}, s32[128]{0:T(128)}, u32[]{:S(2)}) copy-start(s32[128]{0:T(128)} %param.13) | copy-start | bytes 1540
  0.6 68.5 %copy-start = (s32[1024]{0:T(1024)S(1)}, s32[1024]{0:T(1024)}, u32[]{:S(2)}) copy-start(s32[1024]{0:T(1024)} %param.12) | copy-start | bytes 12292

commit v6 on v5

--- a/solution.py
+++ b/solution.py
@@ -253,7 +253,7 @@
     bias_column = jnp.sum(jnp.where(spot == lane, bias[...], 0.0), axis=1, keepdims=True)
     bias_wide[...] = jnp.broadcast_to(bias_column, (rows, LANES))
     x_self[zh, nr] = feats[:, aligned(zh, quarter)]
-    wrow[:, zh, :, aligned(dom, chunk)] = w_both[:, :, aligned(dom, chunk)]
+    wrow[dom, :, zh] = w_both[:, :, aligned(dom, chunk)]
     cot_part[zh] = cot[:, aligned(zh, quarter)]
     bias_part[zh] = bias_wide[...]
     table[pl.ds(own_tiles + 2 * dom, 2)] = picked[dom]
@@ -300,7 +300,7 @@
         )
         targets = (
             x_self.at[source, nr],
-            wrow.at[:, source, :, aligned(dom, chunk)],
+            wrow.at[dom, :, source],
             cot_part.at[source],
             bias_part.at[source],
         )
@@ -329,7 +329,7 @@
     def col_near_copy(i, target):
         return remote(
             w_columns.at[:, :, target],
-            wcol.at[:, :, dom],
+            wcol.at[dom],
             col_s.at[1, i],
             col_near_r,
             {"feat": zh * near + target},
@@ -404,7 +404,7 @@
     x_agg[zh, nr] = agg[:, aligned(zh, quarter)]
 
     def share_copy(which, i, source, target):
-        part = wcol.at[:, :, source] if which else wrow.at[:, :, :, aligned(source, chunk)]
+        part = (wrow, wcol)[which].at[source]
         return remote(part, part, share_s.at[which, i], share_r.at[which, i], {"dom": target})
 
 
@@ -414,7 +414,7 @@
             col_far_copy(i, lax.rem(zh + ZH - i, ZH), zh).wait_recv()
         for i in range(1, near):
             col_near_copy(i, lax.rem(nr + i, near)).start()
-        wcol[:, :, dom] = w_columns[:, :, nr]
+        wcol[dom] = w_columns[:, :, nr]
 
     for i in range(1, ZH):
         far_copy(1, i, lax.rem(zh + ZH - i, ZH), zh).wait_recv()
@@ -440,8 +440,11 @@
         near_copy(0, i, lax.rem(nr + near - i, near), nr).wait_recv()
     for i in range(1, doms):
         share_copy(0, i, lax.rem(dom + doms - i, doms), dom).wait_recv()
+    def row_block(m):
+        return jnp.concatenate([wrow[d, m].reshape(mine, chunk) for d in range(doms)], axis=1)
+
     pre = jnp.dot(
-        wrow[0].reshape(mine, width),
+        row_block(0),
         x_self[...].reshape(width, quarter),
         preferred_element_type=F32,
     )
@@ -453,7 +456,7 @@
     for i in range(1, near):
         near_copy(1, i, lax.rem(nr + near - i, near), nr).wait_recv()
     pre = pre + jnp.dot(
-        wrow[1].reshape(mine, width),
+        row_block(1),
         x_agg[...].reshape(width, quarter),
         preferred_element_type=F32,
     )
@@ -517,7 +520,9 @@
     over_out = (((0,), (0,)), ((), ()))
     for m, target_buffer in ((1, grad_agg), (0, grad_self)):
         back = lax.dot_general(
-            wcol[m].reshape(width, mine),
+            jnp.concatenate(
+                [wcol[n, m, h] for h in range(ZH) for n in range(near)], axis=0
+            ),
             g_all[...].reshape(width, quarter),
             over_out,
             preferred_element_type=F32,
@@ -761,8 +766,8 @@
             pltpu.VMEM((ZH, rows, LANES), F32),
             pltpu.VMEM((rows, columns), BF16),
             pltpu.VMEM((ZH, rows, quarter), BF16),
-            pltpu.VMEM((2, ZH, rows, width), BF16),
-            pltpu.VMEM((2, ZH, near, rows, mine), BF16),
+            pltpu.VMEM((doms, 2, ZH, rows, width // doms), BF16),
+            pltpu.VMEM((near, 2, ZH, rows, mine), BF16),
             pltpu.VMEM((ZH, near, rows, quarter), BF16),
             pltpu.VMEM((ZH, near, rows, quarter), BF16),
             pltpu.VMEM((rows, columns), BF16),

time: 72.2 us -> 72.2 us (level)
  no operation moved by 1% of the time
where the time goes in v6:
time: 72.2 us; the launch traced here: 71.4 us
  Pallas kernels  70.1 us (97%)
  between operations  1.34 us (2%)
    pallas_call x1, Pallas kernels, body(): pl.pallas_call(functools.partial(layer_kernel, doms, near), name='layer',...  68.4 us
    pallas_call x1, Pallas kernels, body(): pl.pallas_call(functools.partial(finish_kernel, doms), name='finish', out...  1.68 us

profile of v6, /device:TPU:1, one launch (start us, length us, event | category | flops | bytes accessed | tf_op | source)
XLA Modules:
  0.0 71.4 jit_solution(14983875416323398735)
XLA Ops:
  0.6 0.0 copy-start.1
  0.6 0.0 copy-start
  1.3 68.4 %layer.1 = (bf16[8,32,128]{2,1,0:T(8,128)(2,1)S(1)}, f32[32,32,128]{2,1,0:T(8,128)S(1)}, bf16[8,2,32,128]{3,2,1,0:T(8,128)(2,1)S(1)}, f32[8,32,256]{2,1,0:T(8,128)S(1)}, f32[32,384]{1,0:T(8,128)S(1)}) custom-call(s32[1]{0:T(128)S(6)} %copy.16.count_ref, bf16[32,4096]{1,0:T(8,128)(2,1)} %feats_hbm.1, s32[8,128]{1,0:T(8,128)} %bitcast.6, s32[1,128]{1,0:T(1,128)} %bitcast.8, ...), custom_call_target="tpu_custom_call" | custom-call | tf_op jit(solution)/shard_map/layer/pallas_call | solution.py:735
  69.7 0.0 copy-done.1
  69.8 0.0 copy-done
  69.8 1.7 %finish.1 = (bf16[32,1024]{1,0:T(8,128)(2,1)}, f32[32,4096]{1,0:T(8,128)}, f32[32,1024]{1,0:T(8,128)}, f32[32,1024]{1,0:T(8,128)}, f32[1,32]{1,0:T(1,128)}) custom-call(f32[32,32,128]{2,1,0:T(8,128)S(1)} %get-tuple-element.15.own_ref, bf16[8,2,32,128]{3,2,1,0:T(8,128)(2,1)S(1)} %get-tuple-element.16.returned_ref, s32[8,128]{1,0:T(8,128)S(1)} %bitcast.7, ...), custom_call_target="tpu_custom_call" | custom-call | tf_op jit(solution)/shard_map/finish/pallas_call | solution.py:830
Async XLA Ops:
  0.6 69.1 %copy-start.1 = (s32[128]{0:T(128)S(1)}, s32[128]{0:T(128)}, u32[]{:S(2)}) copy-start(s32[128]{0:T(128)} %param.13) | copy-start | bytes 1540
  0.6 69.1 %copy-start = (s32[1024]{0:T(1024)S(1)}, s32[1024]{0:T(1024)}, u32[]{:S(2)}) copy-start(s32[1024]{0:T(1024)} %param.12) | copy-start | bytes 12292

commit v7 on v6

--- a/solution.py
+++ b/solution.py
@@ -314,8 +314,6 @@
 
     for i in range(1, ZH):
         far_copy(0, i, zh, lax.rem(zh + i, ZH)).start()
-    for i in range(1, ZH):
-        far_copy(1, i, zh, lax.rem(zh + i, ZH)).start()
 
     def col_far_copy(i, source, target):
         return remote(
@@ -335,11 +333,6 @@
             {"feat": zh * near + target},
         )
 
-    @pl.when(nr == dom)
-    def _():
-        for i in range(1, ZH):
-            col_far_copy(i, zh, lax.rem(zh + i, ZH)).start()
-
 
     for b in range(blocks):
         vals_loads[b].wait()
@@ -367,6 +360,14 @@
     link_copy.wait()
     for i in range(1, doms):
         halo_copy(i, lax.rem(dom + doms - i, doms), dom).wait_recv()
+
+    for i in range(1, ZH):
+        far_copy(1, i, zh, lax.rem(zh + i, ZH)).start()
+
+    @pl.when(nr == dom)
+    def _():
+        for i in range(1, ZH):
+            col_far_copy(i, zh, lax.rem(zh + i, ZH)).start()
 
     runs[tile_total] = jnp.zeros((rows, LANES), F32)
 

time: 72.2 us -> 77.7 us (1.076)
  Pallas kernels: 70.1 us -> 76.3 us
    pallas_call x1, Pallas kernels: 68.4 us -> 74.6 us  [body(): pl.pallas_call(functools.partial(layer_kernel, doms, near), name='layer',...]
where the time goes in v7:
time: 77.7 us; the launch traced here: 77.6 us
  Pallas kernels  76.3 us (98%)
  between operations  1.34 us (2%)
    pallas_call x1, Pallas kernels, body(): pl.pallas_call(functools.partial(layer_kernel, doms, near), name='layer',...  74.6 us
    pallas_call x1, Pallas kernels, body(): pl.pallas_call(functools.partial(finish_kernel, doms), name='finish', out...  1.68 us

profile of v7, /device:TPU:1, one launch (start us, length us, event | category | flops | bytes accessed | tf_op | source)
XLA Modules:
  0.0 77.6 jit_solution(9688543737136036952)
XLA Ops:
  0.6 0.0 copy-start.1
  0.6 0.0 copy-start
  1.3 74.6 %layer.1 = (bf16[8,32,128]{2,1,0:T(8,128)(2,1)S(1)}, f32[32,32,128]{2,1,0:T(8,128)S(1)}, bf16[8,2,32,128]{3,2,1,0:T(8,128)(2,1)S(1)}, f32[8,32,256]{2,1,0:T(8,128)S(1)}, f32[32,384]{1,0:T(8,128)S(1)}) custom-call(s32[1]{0:T(128)S(6)} %copy.16.count_ref, bf16[32,4096]{1,0:T(8,128)(2,1)} %feats_hbm.1, s32[8,128]{1,0:T(8,128)} %bitcast.6, s32[1,128]{1,0:T(1,128)} %bitcast.8, ...), custom_call_target="tpu_custom_call" | custom-call | tf_op jit(solution)/shard_map/layer/pallas_call | solution.py:736
  75.9 0.0 copy-done.1
  75.9 0.0 copy-done
  75.9 1.7 %finish.1 = (bf16[32,1024]{1,0:T(8,128)(2,1)}, f32[32,4096]{1,0:T(8,128)}, f32[32,1024]{1,0:T(8,128)}, f32[32,1024]{1,0:T(8,128)}, f32[1,32]{1,0:T(1,128)}) custom-call(f32[32,32,128]{2,1,0:T(8,128)S(1)} %get-tuple-element.15.own_ref, bf16[8,2,32,128]{3,2,1,0:T(8,128)(2,1)S(1)} %get-tuple-element.16.returned_ref, s32[8,128]{1,0:T(8,128)S(1)} %bitcast.7, ...), custom_call_target="tpu_custom_call" | custom-call | tf_op jit(solution)/shard_map/finish/pallas_call | solution.py:831
Async XLA Ops:
  0.6 75.3 %copy-start.1 = (s32[128]{0:T(128)S(1)}, s32[128]{0:T(128)}, u32[]{:S(2)}) copy-start(s32[128]{0:T(128)} %param.13) | copy-start | bytes 1540
  0.6 75.3 %copy-start = (s32[1024]{0:T(1024)S(1)}, s32[1024]{0:T(1024)}, u32[]{:S(2)}) copy-start(s32[1024]{0:T(1024)} %param.12) | copy-start | bytes 12292
